TPU v7x, 512 devices: a whole 4x8x8 slice. The times are simulated.
512 devices in a mesh: seq: 32 (over z, x), rep: 16 (over y, core).
Axes of the slice: x: 4, y: 8, z: 8, core: 2. Of those that a mesh axis runs over, the one named last changes fastest.
Arguments:
- states: bfloat16 [98304, 512], P(('rep', 'seq')), parts along dimension 0, may hold values from -6 to 6
- starts: int32 [16384], P(('rep', 'seq')), parts along dimension 0, may hold values from 0 to 6143, as said below
- straddle: int32 [512], P(('rep', 'seq')), parts along dimension 0, may hold values from 0 to 63, as said below
- key_weight: bfloat16 [512, 512], replicated
- out_weight: bfloat16 [512, 4096], P(None, 'seq'), may hold values from -0.25 to 0.25
- norm_gain: bfloat16 [4096], P('seq'), may hold values from 0.25 to 1.75
- attn_weight: bfloat16 [4096, 3, 4096], P(None, None, 'seq')
Outputs:
- attended: bfloat16 [16384, 4096], P(('rep', 'seq')), parts along dimension 0
There are 16 independent parts, one for each index of `rep`. A program takes and returns all parts, laid end to end along the dimension named above; an argument that names none is the same for every part. Nothing has to cross between parts.
Inputs may be any that keep to these rules, and one draw needn't show every extreme that they name: Rising; shard s of 192 bytes holds the starts of exactly 32 patches, numbers s * 32 to (s+1) * 32 - 1; the first of them lies at most 63 bytes into the shard, and at byte 0 for shard 0. `straddle`: entry s equals the first start of shard s+1 minus (s+1) * 192; the last entry is 0.
All inputs are finite; a program needn't handle non-finite values.
Results may differ from a plain program's by a relative error of at most 0.0096.
Values may be sent and summed in bfloat16 or wider, within the bound.
No kernel may reach another device: no remote copies, remote signals or barrier semaphores. Data moves between devices by JAX's collectives and lax.ppermute only.
A program may use at most 64 MiB of HBM per device.

v0:
```python
import jax
import jax.numpy as jnp
from jax import lax
from jax.sharding import PartitionSpec as P

HD = 128
LHD = 128
HALO = 64


epsilon = 1e-05


def shifted(shard, axis, by):
    size = lax.axis_size(axis)
    pairs = [(i, i + by) for i in range(size) if 0 <= i + by < size]
    return lax.ppermute(shard, axis, pairs)


def cross_pool(window, local_starts, halo_count, key_weight, patch_total, head_size):
    window_rows = window.shape[0]
    shard_bytes = window_rows - HALO
    width = window.shape[1]
    head_count = width // head_size
    position = jnp.arange(window_rows, dtype=jnp.int32)
    patch_ends = jnp.concatenate([local_starts[1:], (shard_bytes + halo_count).reshape(1)])
    member = (position[None, :] >= local_starts[:, None]) & (
        position[None, :] < patch_ends[:, None]
    )
    byte_count = jnp.sum(member.astype(jnp.float32), axis=1)
    query = (
        jnp.dot(member.astype(jnp.bfloat16), window, preferred_element_type=jnp.float32)
        / byte_count[:, None]
    ).astype(jnp.bfloat16)
    keys = jnp.dot(window, key_weight, preferred_element_type=jnp.float32).astype(jnp.bfloat16)
    query_heads = query.reshape(patch_total, head_count, head_size)
    key_heads = keys.reshape(window_rows, head_count, head_size)
    scores = jnp.einsum(
        "phd,jhd->hpj", query_heads, key_heads, preferred_element_type=jnp.float32
    ) / jnp.sqrt(jnp.float32(head_size))
    scores = jnp.where(member[None], scores, jnp.float32(-1e30))
    row_peak = jnp.max(scores, axis=-1, keepdims=True)
    expo = jnp.where(member[None], jnp.exp(scores - row_peak), jnp.float32(0.0))
    cross = (expo / jnp.sum(expo, axis=-1, keepdims=True)).astype(jnp.bfloat16)
    value_heads = window.reshape(window_rows, head_count, head_size)
    pooled = jnp.einsum("hpj,jhd->phd", cross, value_heads, preferred_element_type=jnp.float32)
    return pooled.reshape(patch_total, width).astype(jnp.bfloat16)


def global_attend(head_view):
    patch_count = head_view.shape[0]
    scores = jnp.einsum(
        "qhd,khd->hqk", head_view[:, 0], head_view[:, 1], preferred_element_type=jnp.float32
    ) / jnp.sqrt(jnp.float32(HD))
    causal = jnp.arange(patch_count)[:, None] >= jnp.arange(patch_count)[None, :]
    scores = jnp.where(causal[None], scores, jnp.float32(-1e30))
    row_peak = jnp.max(scores, axis=-1, keepdims=True)
    expo = jnp.where(causal[None], jnp.exp(scores - row_peak), jnp.float32(0.0))
    probs = (expo / jnp.sum(expo, axis=-1, keepdims=True)).astype(jnp.bfloat16)
    attended = jnp.einsum(
        "hqk,khd->qhd", probs, head_view[:, 2], preferred_element_type=jnp.float32
    )
    return attended.reshape(patch_count, head_view.shape[2] * HD).astype(jnp.bfloat16)


def norm_rows(embedding, gain_row):
    meansq = jnp.mean(embedding * embedding, axis=1, keepdims=True)
    return (embedding * lax.rsqrt(meansq + epsilon) * gain_row.astype(jnp.float32)).astype(
        jnp.bfloat16
    )


def shards(states, starts, straddle, key_weight, out_weight, norm_gain, attn_weight):
    shard_index = lax.axis_index("seq")
    byte_rows = states.shape[0]
    patch_local = starts.shape[0]
    halo_rows = shifted(states[:HALO], "seq", -1)
    window = jnp.concatenate([states, halo_rows], axis=0)
    local_starts = starts - shard_index * byte_rows
    pooled = cross_pool(window, local_starts, straddle[0], key_weight, patch_local, LHD)
    local_width = attn_weight.shape[2]
    model_width = attn_weight.shape[0]
    proj_weight = attn_weight.reshape(model_width, 3 * local_width)
    out_full, gain_full = (
        lax.all_gather(out_weight, "seq", axis=1, tiled=True),
        lax.all_gather(norm_gain.reshape(1, -1), "seq", axis=1, tiled=True),
    )
    embedding = jnp.dot(pooled, out_full, preferred_element_type=jnp.float32)
    normed = norm_rows(embedding, gain_full)
    projected = jnp.dot(
        lax.all_gather(normed, "seq", axis=0, tiled=True),
        proj_weight,
        preferred_element_type=jnp.float32,
    ).astype(jnp.bfloat16)
    head_view = projected.reshape(projected.shape[0], 3, local_width // HD, HD)
    attended = global_attend(head_view)
    return lax.all_to_all(attended, "seq", split_axis=0, concat_axis=1, tiled=True)


def solution(mesh):
    placed = (
        P(("rep", "seq"), None),
        P(("rep", "seq")),
        P(("rep", "seq")),
        P(),
        P(None, "seq"),
        P("seq"),
        P(None, None, "seq"),
    )
    return jax.shard_map(
        shards, mesh=mesh, in_specs=placed, out_specs=P(("rep", "seq"), None), check_vma=False
    )
```

profile of v0, /device:TPU:1, one launch (start us, length us, event | category | flops | bytes accessed | tf_op | source)
XLA Modules:
  0.0 245.5 jit_solution(9140741254961553201)
XLA Ops:
  6.5 0.0 copy-start
  6.5 0.0 all-gather.5.cloned.1.call-start
  6.5 0.7 all-gather.5.cloned.1.call-update
  7.3 0.0 all-gather.7.cloned.1.call-start
  7.3 1.1 copy.29
  8.4 1.3 collective-permute-start
  10.3 0.7 broadcast_subtract_fusion
  11.0 0.1 slice.16
  11.1 40.8 %all-gather.1 = bf16[32,1,128]{2,1,0:T(2,128)(2,1)S(1)} all-gather(bf16[1,1,128]{2,1,0:T(2,128)(2,1)} %bitcast.62), channel_id=2, replica_groups=mesh['seq'=32,'rep'=16] {'seq'}, dimensions={0}, use_global_device_ids=true | all-gather | bytes 8448 | tf_op jit(solution)/shard_map/all_gather | solution.py:86
  51.9 0.1 pad_add_fusion
  52.0 0.1 fusion.23
  52.1 0.2 convert_reduce_fusion
  52.3 0.0 collective-permute-done
  52.3 0.1 pad_maximum_fusion
  52.4 0.2 fusion.13
  52.6 0.0 copy-done
  52.6 0.3 fusion.5
  52.9 0.4 fusion.28
  53.3 0.2 fusion.12
  53.5 48.5 %all-gather.5.cloned.1.call-done = bf16[512,4096]{1,0:T(8,128)(2,1)} async-done(((bf16[512,128]{1,0:T(8,128)(2,1)}), bf16[512,4096]{1,0:T(8,128)(2,1)}) %all-gather.5.cloned.1.call-update) | async-done | bytes 4194320 | tf_op jit(solution)/shard_map/all_gather | solution.py:85
  102.0 3.1 %multiply_reduce_fusion = (f32[32]{0:T(128)S(1)}, f32[32,4096]{1,0:T(8,128)S(1)}) fusion(bf16[512,4096]{1,0:T(8,128)(2,1)} %all-gather.5.cloned.1.call-done, bf16[4,4,8,128]{3,2,1,0:T(8,128)(2,1)S(1)} %fusion.12), kind=kOutput, calls=%fused_computation.24 | convolution fusion | flops 134479840 | bytes 4751488 | tf_op jit(solution)/shard_map/dot_general | solution.py:88
  105.1 0.8 multiply_convert_fusion
  106.0 0.0 all-gather.7.cloned.1.call-update
  106.0 4.7 %copy.34 = bf16[4096,3,128]{0,2,1:T(8,128)(2,1)} copy(bf16[4096,3,128]{2,0,1:T(8,128)(2,1)} %param.13) | data formatting | bytes 6291456 | tf_op args[6]
  110.7 101.9 %all-gather.7.cloned.1.call-done = bf16[1024,4096]{1,0:T(8,128)(2,1)} async-done(((bf16[32,4096]{1,0:T(8,128)(2,1)}), bf16[1024,4096]{1,0:T(8,128)(2,1)}) %all-gather.7.cloned.1.call-update) | async-done | bytes 8388624 | tf_op jit(solution)/shard_map/all_gather | solution.py:91
  212.6 7.7 %convolution_convert_fusion = bf16[1024,384]{0,1:T(8,128)(2,1)S(1)} fusion(bf16[1024,4096]{1,0:T(8,128)(2,1)} %all-gather.7.cloned.1.call-done, bf16[4096,384]{0,1:T(8,128)(2,1)} %bitcast.58), kind=kOutput, calls=%fused_computation.8 | convolution fusion | flops 3221618688 | bytes 12320768 | tf_op jit(solution)/shard_map/dot_general | solution.py:90
  220.4 0.8 fusion.1
  221.1 0.5 fusion.2
  221.6 0.8 fusion.6
  222.4 0.2 copy.35
  222.5 15.4 %all_to_all.16 = bf16[32,32,128]{2,1,0:T(8,128)(2,1)S(1)} all-to-all(bf16[32,32,128]{2,1,0:T(8,128)(2,1)S(1)} %bitcast.59), channel_id=1, replica_groups=mesh['seq'=32,'rep'=16] {'seq'}, dimensions={0} | all-to-all | bytes 524288 | tf_op jit(solution)/shard_map/all_to_all | solution.py:97
  237.9 0.7 copy_bitcast_fusion
  (3 shorter events, 0.0 us)
Async XLA Ops:
  6.5 46.1 %copy-start = (bf16[512,512]{1,0:T(8,128)(2,1)S(1)}, bf16[512,512]{1,0:T(8,128)(2,1)}, u32[]{:S(2)}) copy-start(bf16[512,512]{1,0:T(8,128)(2,1)} %param.10) | copy-start | bytes 1572868
  6.5 95.5 %all-gather.5.cloned.1.call-start = ((), (), s32[]{:S(2)}) async-start(), calls=%async_computation.1 | async-start | bytes 4325376 | tf_op jit(solution)/shard_map/all_gather | solution.py:85
  7.3 205.4 %all-gather.7.cloned.1.call-start = ((), (), s32[]{:S(2)}) async-start(), calls=%async_computation.2 | async-start | bytes 8650752 | tf_op jit(solution)/shard_map/all_gather | solution.py:91
  8.4 43.9 %collective-permute-start = (bf16[64,512]{0,1:T(8,128)(2,1)S(1)}, bf16[64,512]{0,1:T(8,128)(2,1)S(1)}, u32[]{:S(2)}, u32[]{:S(2)}) collective-permute-start(bf16[64,512]{0,1:T(8,128)(2,1)S(1)} %slice.20), channel_id=1, source_target_pairs={{16,0},{32,16},{48,32},{64,48},{80,64},{96,80},{112,96},{128,112},... | collective-permute-start | bytes 196616 | tf_op jit(solution)/shard_map/ppermute | solution.py:17
Sparse Core Ops, SparseCore 0:
  10.4 91.5 all-gather.4
  106.1 106.4 all-gather.6
where the time goes:
time: 248 us; the launch traced here: 245 us
  waiting for transfers between devices  151 us (61%)
  blocking collectives  56.2 us (23%)
  between operations  14.2 us (6%)
  matrix products  13.4 us (5%)
  local copies, waits for them, and re-layouts  6.75 us (3%)
    all_gather x1, waiting for transfers between devices, shards(): lax.all_gather(normed, 'seq', axis=0, tiled=True)  102 us
    all_gather x1, waiting for transfers between devices, shards(): lax.all_gather(out_weight, 'seq', axis=1, tiled=True)  48.5 us
    all_gather x1, blocking collectives, shards(): lax.all_gather(norm_gain.reshape(1, -1), 'seq', axis=1, tiled=True)  40.8 us
    all_to_all x1, blocking collectives, shards(): lax.all_to_all(attended, 'seq', split_axis=0, concat_axis=1, tiled=True)  15.4 us
    dot_general x1, matrix products, shards(): jnp.dot(lax.all_gather(normed, 'seq', axis=0, tiled=True), proj_weight, p...  7.71 us
    unnamed x4, local copies, waits for them, and re-layouts  5.78 us
  transfers between devices with their start and end apart: 3, of which 2 were waited for; matrix products, arithmetic and copies ran while one was open for 3% of the time, Pallas kernels for 0%

commit v1 on v0

--- a/solution.py
+++ b/solution.py
@@ -63,34 +63,51 @@
     return attended.reshape(patch_count, head_view.shape[2] * HD).astype(jnp.bfloat16)
 
 
-def norm_rows(embedding, gain_row):
-    meansq = jnp.mean(embedding * embedding, axis=1, keepdims=True)
-    return (embedding * lax.rsqrt(meansq + epsilon) * gain_row.astype(jnp.float32)).astype(
-        jnp.bfloat16
-    )
+def spread(block, axis):
+    copies = jnp.broadcast_to(block[None], (lax.axis_size(axis),) + block.shape)
+    return lax.all_to_all(copies, axis, split_axis=0, concat_axis=0, tiled=True)
 
 
 def shards(states, starts, straddle, key_weight, out_weight, norm_gain, attn_weight):
     shard_index = lax.axis_index("seq")
     byte_rows = states.shape[0]
     patch_local = starts.shape[0]
+    local_width = attn_weight.shape[2]
+    model_width = attn_weight.shape[0]
+    pooled_width = out_weight.shape[0]
+
+    piece = pooled_width // lax.axis_size("rep")
+    rows = lax.dynamic_slice_in_dim(out_weight, lax.axis_index("rep") * piece, piece, 0)
+    gain_block = jnp.broadcast_to(norm_gain[None], (8, norm_gain.shape[0]))
+    weight_blocks = spread(jnp.concatenate([rows, gain_block], axis=0), "seq")
+    row_block = weight_blocks[:, :piece].astype(jnp.float32)
+    gain = weight_blocks[:, piece : piece + 1].astype(jnp.float32)
+    scaled = jnp.swapaxes(row_block * gain, 0, 1).reshape(piece, model_width)
+    scaled_high = scaled.astype(jnp.bfloat16)
+    scaled_low = (scaled - scaled_high.astype(jnp.float32)).astype(jnp.bfloat16)
+    proj_weight = attn_weight.reshape(model_width, 3 * local_width)
+    merged = jnp.dot(
+        jnp.concatenate([scaled_high, scaled_low], axis=0),
+        proj_weight,
+        preferred_element_type=jnp.float32,
+    )
+    merged = (merged[:piece] + merged[piece:]).astype(jnp.bfloat16)
+    merged_all = spread(merged, "rep").reshape(pooled_width, 3 * local_width)
+
     halo_rows = shifted(states[:HALO], "seq", -1)
     window = jnp.concatenate([states, halo_rows], axis=0)
     local_starts = starts - shard_index * byte_rows
     pooled = cross_pool(window, local_starts, straddle[0], key_weight, patch_local, LHD)
-    local_width = attn_weight.shape[2]
-    model_width = attn_weight.shape[0]
-    proj_weight = attn_weight.reshape(model_width, 3 * local_width)
-    out_full, gain_full = (
-        lax.all_gather(out_weight, "seq", axis=1, tiled=True),
-        lax.all_gather(norm_gain.reshape(1, -1), "seq", axis=1, tiled=True),
+    pooled_all = spread(pooled, "seq").reshape(-1, pooled_width)
+
+    part = lax.dot_general(
+        out_weight, pooled_all, (((0,), (1,)), ((), ())), preferred_element_type=jnp.float32
     )
-    embedding = jnp.dot(pooled, out_full, preferred_element_type=jnp.float32)
-    normed = norm_rows(embedding, gain_full)
-    projected = jnp.dot(
-        lax.all_gather(normed, "seq", axis=0, tiled=True),
-        proj_weight,
-        preferred_element_type=jnp.float32,
+    part_square = jnp.sum(part * part, axis=0).reshape(-1, 128)
+    square = jnp.sum(spread(part_square, "seq"), axis=0).reshape(-1)
+    inverse = lax.rsqrt(square / model_width + epsilon)
+    projected = (
+        jnp.dot(pooled_all, merged_all, preferred_element_type=jnp.float32) * inverse[:, None]
     ).astype(jnp.bfloat16)
     head_view = projected.reshape(projected.shape[0], 3, local_width // HD, HD)
     attended = global_attend(head_view)

time: 248 us -> 126 us (0.51)
  waiting for transfers between devices: 151 us -> 51.2 us
  blocking collectives: 56.2 us -> 15.9 us
  starting transfers between devices: 1.33 us -> 37.8 us
  between operations: 14.2 us -> 0.83 us
  matrix products: 13.4 us -> 6.7 us
  local copies, waits for them, and re-layouts: 6.75 us -> 11.5 us
    all_gather x2 -> x0, waiting for transfers between devices: 150 us -> none  [the longest x1 102 us: shards(): lax.all_gather(normed, 'seq', axis=0, tiled=True)]
    all_to_all x0 -> x4, waiting for transfers between devices: none -> 51.2 us  [spread(): return lax.all_to_all(copies, axis, split_axis=0, concat_axis=0, tiled=True)]
    all_gather x1 -> x0, blocking collectives: 40.8 us -> none  [shards(): lax.all_gather(norm_gain.reshape(1, -1), 'seq', axis=1, tiled=True)]
    all_to_all x0 -> x4, starting transfers between devices: none -> 36.5 us  [spread(): return lax.all_to_all(copies, axis, split_axis=0, concat_axis=0, tiled=True)]
    dot_general x2 -> x3, matrix products: 10.8 us -> 4.08 us  [the longest x1 2.97 us: shards(): jnp.dot(jnp.concatenate([scaled_high, scaled_low], axis=0), proj_weight,...]
    broadcast_in_dim x0 -> x5, local copies, waits for them, and re-layouts: none -> 3.96 us  [the longest x4 3.3 us: spread(): copies = jnp.broadcast_to(block[None], (lax.axis_size(axis),) + block.shape)]
    unnamed x4 -> x6, local copies, waits for them, and re-layouts: 5.78 us -> 5.82 us
  transfers between devices with their start and end apart: 3 -> 5, of which waited for: 2 -> 4; matrix products, arithmetic and copies ran while one was open for 3% -> 10% of each run, Pallas kernels for 0% -> 0%
where the time goes in v1:
time: 126 us
  waiting for transfers between devices  51.2 us (41%)
  starting transfers between devices  37.8 us (30%)
  blocking collectives  15.9 us (13%)
  local copies, waits for them, and re-layouts  11.5 us (9%)
  matrix products  6.7 us (5%)
  other arithmetic  1.77 us (1%)
    all_to_all x4, waiting for transfers between devices, spread(): return lax.all_to_all(copies, axis, split_axis=0, concat_axis=0, tiled=True)  51.2 us
    all_to_all x4, starting transfers between devices, spread(): return lax.all_to_all(copies, axis, split_axis=0, concat_axis=0, tiled=True)  36.5 us
    all_to_all x1, blocking collectives, shards(): lax.all_to_all(attended, 'seq', split_axis=0, concat_axis=1, tiled=True)  15.9 us
    unnamed x6, local copies, waits for them, and re-layouts  5.82 us
    broadcast_in_dim x4, local copies, waits for them, and re-layouts, spread(): copies = jnp.broadcast_to(block[None], (lax.axis_size(axis),) + block.shape)  3.3 us
    dot_general x1, matrix products, shards(): jnp.dot(jnp.concatenate([scaled_high, scaled_low], axis=0), proj_weight,...  2.97 us
  transfers between devices with their start and end apart: 5, of which 4 were waited for; matrix products, arithmetic and copies ran while one was open for 10% of the time, Pallas kernels for 0%

profile of v1, /device:TPU:1, one launch (start us, length us, event | category | flops | bytes accessed | tf_op | source)
XLA Modules:
  0.0 125.7 jit_solution(8662228639013274405)
XLA Ops:
  0.0 0.0 copy-start
  0.0 1.1 copy.39
  1.1 1.3 %collective-permute-start = (bf16[64,512]{0,1:T(8,128)(2,1)S(1)}, bf16[64,512]{0,1:T(8,128)(2,1)S(1)}, u32[]{:S(2)}, u32[]{:S(2)}) collective-permute-start(bf16[64,512]{0,1:T(8,128)(2,1)S(1)} %slice.36), channel_id=1, source_target_pairs={{16,0},{32,16},{48,32},{64,48},{80,64},{96,80},{112,96},{128,112},... | collective-permute-start | bytes 196616 | tf_op jit(solution)/shard_map/ppermute | solution.py:17
  2.5 0.7 constant_dynamic-slice_fusion
  3.2 0.7 broadcast_in_dim.40
  3.8 0.8 broadcast_in_dim.42
  4.6 14.6 %all-to-all-start.1 = ((bf16[32,40,128]{2,1,0:T(8,128)(2,1)}), bf16[32,40,128]{2,1,0:T(8,128)(2,1)S(1)}, u32[]{:S(2)}, u32[]{:S(2)}) async-start(bf16[32,40,128]{2,1,0:T(8,128)(2,1)} %broadcast_in_dim.42), calls=%async_computation.1 | async-start | bytes 655360 | tf_op jit(solution)/shard_map/all_to_all | solution.py:68
  19.8 0.7 broadcast_subtract_fusion
  20.5 0.1 slice.28
  20.6 0.1 pad_add_fusion
  20.7 0.1 fusion.27
  20.7 4.7 %copy.45 = bf16[4096,3,128]{0,2,1:T(8,128)(2,1)} copy(bf16[4096,3,128]{2,0,1:T(8,128)(2,1)} %param.13) | data formatting | bytes 6291456 | tf_op args[6]
  25.4 0.0 copy-start.1
  25.4 0.2 convert_reduce_fusion
  25.6 0.0 collective-permute-done
  25.6 0.1 pad_maximum_fusion
  25.7 0.2 fusion.14
  25.9 0.0 copy-done
  26.0 0.3 fusion.6
  26.3 0.4 fusion.33
  26.6 0.2 fusion.13
  26.9 4.8 %all-to-all-done.1 = bf16[32,40,128]{2,1,0:T(8,128)(2,1)S(1)} async-done(((bf16[32,40,128]{2,1,0:T(8,128)(2,1)}), bf16[32,40,128]{2,1,0:T(8,128)(2,1)S(1)}, u32[]{:S(2)}, u32[]{:S(2)}) %all-to-all-start.1) | async-done | bytes 327712 | tf_op jit(solution)/shard_map/all_to_all | solution.py:68
  31.7 1.1 broadcast_in_dim.39
  32.8 4.8 %all-to-all-start = ((bf16[32,32,512]{2,1,0:T(8,128)(2,1)}), bf16[32,32,512]{2,1,0:T(8,128)(2,1)S(1)}, u32[]{:S(2)}, u32[]{:S(2)}) async-start(bf16[32,32,512]{2,1,0:T(8,128)(2,1)} %broadcast_in_dim.39), calls=%async_computation | async-start | bytes 2097152 | tf_op jit(solution)/shard_map/all_to_all | solution.py:68
  37.7 0.1 fusion.15
  37.8 25.5 %all-to-all-done = bf16[32,32,512]{2,1,0:T(8,128)(2,1)S(1)} async-done(((bf16[32,32,512]{2,1,0:T(8,128)(2,1)}), bf16[32,32,512]{2,1,0:T(8,128)(2,1)S(1)}, u32[]{:S(2)}, u32[]{:S(2)}) %all-to-all-start) | async-done | bytes 1048608 | tf_op jit(solution)/shard_map/all_to_all | solution.py:68
  63.3 0.0 copy-done.1
  63.3 0.5 fusion.5
  63.8 0.7 broadcast_in_dim.80
  64.5 6.7 %all-to-all-start.3 = ((f32[32,8,128]{2,1,0:T(8,128)}), f32[32,8,128]{2,1,0:T(8,128)S(1)}, u32[]{:S(2)}, u32[]{:S(2)}) async-start(f32[32,8,128]{2,1,0:T(8,128)} %broadcast_in_dim.80), calls=%async_computation.3 | async-start | bytes 262144 | tf_op jit(solution)/shard_map/all_to_all | solution.py:68
  71.1 3.0 %fusion.16 = f32[64,384]{1,0:T(8,128)S(1)} fusion(bf16[4096,384]{0,1:T(8,128)(2,1)} %bitcast.74, bf16[32,4096]{1,0:T(8,128)(2,1)S(1)} %fusion.15, bf16[32,4096]{1,0:T(8,128)(2,1)S(1)} %bitcast_convert_fusion), kind=kOutput, calls=%fused_computation.28 | convolution fusion | flops 202375168 | bytes 3768320 | tf_op jit(solution)/shard_map/dot_general | solution.py:89
  74.1 6.4 %all-to-all-done.3 = f32[32,8,128]{2,1,0:T(8,128)S(1)} async-done(((f32[32,8,128]{2,1,0:T(8,128)}), f32[32,8,128]{2,1,0:T(8,128)S(1)}, u32[]{:S(2)}, u32[]{:S(2)}) %all-to-all-start.3) | async-done | bytes 131104 | tf_op jit(solution)/shard_map/all_to_all | solution.py:68
  80.6 0.8 broadcast_in_dim.43
  81.4 10.4 %all-to-all-start.2 = ((bf16[16,32,384]{2,1,0:T(8,128)(2,1)}), bf16[16,32,384]{2,1,0:T(8,128)(2,1)S(1)}, u32[]{:S(2)}, u32[]{:S(2)}) async-start(bf16[16,32,384]{2,1,0:T(8,128)(2,1)} %broadcast_in_dim.43), calls=%async_computation.2 | async-start | bytes 786432 | tf_op jit(solution)/shard_map/all_to_all | solution.py:68
  91.8 14.4 %all-to-all-done.2 = bf16[16,32,384]{2,1,0:T(8,128)(2,1)S(1)} async-done(((bf16[16,32,384]{2,1,0:T(8,128)(2,1)}), bf16[16,32,384]{2,1,0:T(8,128)(2,1)S(1)}, u32[]{:S(2)}, u32[]{:S(2)}) %all-to-all-start.2) | async-done | bytes 393248 | tf_op jit(solution)/shard_map/all_to_all | solution.py:68
  106.3 0.6 multiply_convert_fusion
  106.9 0.8 fusion.1
  107.7 0.5 fusion.2
  108.2 0.8 fusion.7
  108.9 0.2 copy.46
  109.1 15.9 %all_to_all.36 = bf16[32,32,128]{2,1,0:T(8,128)(2,1)S(1)} all-to-all(bf16[32,32,128]{2,1,0:T(8,128)(2,1)S(1)} %bitcast.77), channel_id=1, replica_groups=mesh['seq'=32,'rep'=16] {'seq'}, dimensions={0} | all-to-all | bytes 524288 | tf_op jit(solution)/shard_map/all_to_all | solution.py:114
  125.0 0.7 copy_bitcast_fusion
  (8 shorter events, 0.2 us)
Async XLA Ops:
  0.0 25.9 %copy-start = (bf16[512,512]{1,0:T(8,128)(2,1)S(1)}, bf16[512,512]{1,0:T(8,128)(2,1)}, u32[]{:S(2)}) copy-start(bf16[512,512]{1,0:T(8,128)(2,1)} %param.10) | copy-start | bytes 1572868
  1.1 24.5 %collective-permute-start = (bf16[64,512]{0,1:T(8,128)(2,1)S(1)}, bf16[64,512]{0,1:T(8,128)(2,1)S(1)}, u32[]{:S(2)}, u32[]{:S(2)}) collective-permute-start(bf16[64,512]{0,1:T(8,128)(2,1)S(1)} %slice.36), channel_id=1, source_target_pairs={{16,0},{32,16},{48,32},{64,48},{80,64},{96,80},{112,96},{128,112},... | collective-permute-start | bytes 196616 | tf_op jit(solution)/shard_map/ppermute | solution.py:17
  4.6 27.1 %all-to-all-start.1 = ((bf16[32,40,128]{2,1,0:T(8,128)(2,1)}), bf16[32,40,128]{2,1,0:T(8,128)(2,1)S(1)}, u32[]{:S(2)}, u32[]{:S(2)}) async-start(bf16[32,40,128]{2,1,0:T(8,128)(2,1)} %broadcast_in_dim.42), calls=%async_computation.1 | async-start | bytes 655360 | tf_op jit(solution)/shard_map/all_to_all | solution.py:68
  25.4 37.9 %copy-start.1 = (bf16[512,128]{1,0:T(8,128)(2,1)S(1)}, bf16[512,128]{1,0:T(8,128)(2,1)}, u32[]{:S(2)}) copy-start(bf16[512,128]{1,0:T(8,128)(2,1)} %param.11) | copy-start | bytes 393220
  32.8 30.5 %all-to-all-start = ((bf16[32,32,512]{2,1,0:T(8,128)(2,1)}), bf16[32,32,512]{2,1,0:T(8,128)(2,1)S(1)}, u32[]{:S(2)}, u32[]{:S(2)}) async-start(bf16[32,32,512]{2,1,0:T(8,128)(2,1)} %broadcast_in_dim.39), calls=%async_computation | async-start | bytes 2097152 | tf_op jit(solution)/shard_map/all_to_all | solution.py:68
  64.5 16.1 %all-to-all-start.3 = ((f32[32,8,128]{2,1,0:T(8,128)}), f32[32,8,128]{2,1,0:T(8,128)S(1)}, u32[]{:S(2)}, u32[]{:S(2)}) async-start(f32[32,8,128]{2,1,0:T(8,128)} %broadcast_in_dim.80), calls=%async_computation.3 | async-start | bytes 262144 | tf_op jit(solution)/shard_map/all_to_all | solution.py:68
  81.4 24.9 %all-to-all-start.2 = ((bf16[16,32,384]{2,1,0:T(8,128)(2,1)}), bf16[16,32,384]{2,1,0:T(8,128)(2,1)S(1)}, u32[]{:S(2)}, u32[]{:S(2)}) async-start(bf16[16,32,384]{2,1,0:T(8,128)(2,1)} %broadcast_in_dim.43), calls=%async_computation.2 | async-start | bytes 786432 | tf_op jit(solution)/shard_map/all_to_all | solution.py:68

commit v2 on v1

--- a/solution.py
+++ b/solution.py
@@ -2,6 +2,7 @@
 import jax.numpy as jnp
 from jax import lax
 from jax.sharding import PartitionSpec as P
+
 
 HD = 128
 LHD = 128
@@ -68,48 +69,56 @@
     return lax.all_to_all(copies, axis, split_axis=0, concat_axis=0, tiled=True)
 
 
-def shards(states, starts, straddle, key_weight, out_weight, norm_gain, attn_weight):
+def weight_rows(out_weight, norm_gain):
+    piece = out_weight.shape[0] // lax.axis_size("rep")
+    rows = lax.dynamic_slice_in_dim(out_weight, lax.axis_index("rep") * piece, piece, 0)
+    gain_block = jnp.broadcast_to(norm_gain[None], (8, norm_gain.shape[0]))
+    return jnp.concatenate([rows, gain_block], axis=0)
+
+
+def merge_weights(weight_blocks, attn_weight):
+    model_width = attn_weight.shape[0]
+    piece = weight_blocks.shape[1] - 8
+    row_block = weight_blocks[:, :piece].astype(jnp.float32)
+    gain = weight_blocks[:, piece : piece + 1].astype(jnp.float32)
+    scaled = jnp.swapaxes(row_block * gain, 0, 1).reshape(piece, model_width)
+    high = scaled.astype(jnp.bfloat16)
+    low = (scaled - high.astype(jnp.float32)).astype(jnp.bfloat16)
+    both = jnp.concatenate([high, low], axis=0)
+    merged = [
+        jnp.dot(both, attn_weight[:, part], preferred_element_type=jnp.float32)
+        for part in range(3)
+    ]
+    merged = jnp.concatenate([m[:piece] + m[piece:] for m in merged], axis=1)
+    return merged.astype(jnp.bfloat16)
+
+
+def layer(states, starts, straddle, key_weight, out_weight, norm_gain, attn_weight):
     shard_index = lax.axis_index("seq")
     byte_rows = states.shape[0]
     patch_local = starts.shape[0]
-    local_width = attn_weight.shape[2]
     model_width = attn_weight.shape[0]
     pooled_width = out_weight.shape[0]
 
-    piece = pooled_width // lax.axis_size("rep")
-    rows = lax.dynamic_slice_in_dim(out_weight, lax.axis_index("rep") * piece, piece, 0)
-    gain_block = jnp.broadcast_to(norm_gain[None], (8, norm_gain.shape[0]))
-    weight_blocks = spread(jnp.concatenate([rows, gain_block], axis=0), "seq")
-    row_block = weight_blocks[:, :piece].astype(jnp.float32)
-    gain = weight_blocks[:, piece : piece + 1].astype(jnp.float32)
-    scaled = jnp.swapaxes(row_block * gain, 0, 1).reshape(piece, model_width)
-    scaled_high = scaled.astype(jnp.bfloat16)
-    scaled_low = (scaled - scaled_high.astype(jnp.float32)).astype(jnp.bfloat16)
-    proj_weight = attn_weight.reshape(model_width, 3 * local_width)
-    merged = jnp.dot(
-        jnp.concatenate([scaled_high, scaled_low], axis=0),
-        proj_weight,
-        preferred_element_type=jnp.float32,
-    )
-    merged = (merged[:piece] + merged[piece:]).astype(jnp.bfloat16)
-    merged_all = spread(merged, "rep").reshape(pooled_width, 3 * local_width)
-
+    weight_blocks = spread(weight_rows(out_weight, norm_gain), "seq")
     halo_rows = shifted(states[:HALO], "seq", -1)
     window = jnp.concatenate([states, halo_rows], axis=0)
     local_starts = starts - shard_index * byte_rows
     pooled = cross_pool(window, local_starts, straddle[0], key_weight, patch_local, LHD)
     pooled_all = spread(pooled, "seq").reshape(-1, pooled_width)
-
+    merged = merge_weights(weight_blocks, attn_weight)
+    merged_all = lax.all_gather(merged, "rep", axis=0, tiled=True)
     part = lax.dot_general(
         out_weight, pooled_all, (((0,), (1,)), ((), ())), preferred_element_type=jnp.float32
     )
     part_square = jnp.sum(part * part, axis=0).reshape(-1, 128)
-    square = jnp.sum(spread(part_square, "seq"), axis=0).reshape(-1)
+    square_all = spread(part_square, "seq")
+    square = jnp.sum(square_all, axis=0).reshape(-1)
     inverse = lax.rsqrt(square / model_width + epsilon)
     projected = (
         jnp.dot(pooled_all, merged_all, preferred_element_type=jnp.float32) * inverse[:, None]
     ).astype(jnp.bfloat16)
-    head_view = projected.reshape(projected.shape[0], 3, local_width // HD, HD)
+    head_view = projected.reshape(projected.shape[0], 3, -1, HD)
     attended = global_attend(head_view)
     return lax.all_to_all(attended, "seq", split_axis=0, concat_axis=1, tiled=True)
 
@@ -125,5 +134,5 @@
         P(None, None, "seq"),
     )
     return jax.shard_map(
-        shards, mesh=mesh, in_specs=placed, out_specs=P(("rep", "seq"), None), check_vma=False
+        layer, mesh=mesh, in_specs=placed, out_specs=P(("rep", "seq"), None), check_vma=False
     )

time: 126 us -> 117 us (0.929)
  blocking collectives: 15.9 us -> 41.7 us
  waiting for transfers between devices: 51.2 us -> 30.4 us
  starting transfers between devices: 37.8 us -> 27.3 us
  local copies, waits for them, and re-layouts: 11.5 us -> 6.02 us
  matrix products: 6.7 us -> 8.35 us
    all_to_all x4 -> x3, waiting for transfers between devices: 51.2 us -> 30.4 us  [spread(): return lax.all_to_all(copies, axis, split_axis=0, concat_axis=0, tiled=True)]
    all_gather x0 -> x1, blocking collectives: none -> 20.7 us  [layer(): merged_all = lax.all_gather(merged, 'rep', axis=0, tiled=True)]
    all_to_all x4 -> x3, starting transfers between devices: 36.5 us -> 26 us  [spread(): return lax.all_to_all(copies, axis, split_axis=0, concat_axis=0, tiled=True)]
    all_to_all x1, blocking collectives: 15.9 us -> 20.9 us  [layer(): lax.all_to_all(attended, 'seq', split_axis=0, concat_axis=1, tiled=True)]
    unnamed x6 -> x5, local copies, waits for them, and re-layouts: 5.82 us -> 1.13 us
    dot_general x3 -> x5, matrix products: 4.08 us -> 5.73 us  [the longest x3 4.62 us: merge_weights(): jnp.dot(both, attn_weight[:, part], preferred_element_type=jnp.float32)]
    broadcast_in_dim x4 -> x3, local copies, waits for them, and re-layouts: 3.3 us -> 2.53 us  [spread(): copies = jnp.broadcast_to(block[None], (lax.axis_size(axis),) + block.shape)]
  transfers between devices with their start and end apart: 5 -> 4, of which waited for: 4 -> 2; matrix products, arithmetic and copies ran while one was open for 10% -> 8% of each run, Pallas kernels for 0% -> 0%
where the time goes in v2:
time: 117 us; the launch traced here: 116 us
  blocking collectives  41.7 us (36%)
  waiting for transfers between devices  30.4 us (26%)
  starting transfers between devices  27.3 us (23%)
  matrix products  8.35 us (7%)
  local copies, waits for them, and re-layouts  6.02 us (5%)
  other arithmetic  1.78 us (2%)
    all_to_all x3, waiting for transfers between devices, spread(): return lax.all_to_all(copies, axis, split_axis=0, concat_axis=0, tiled=True)  30.4 us
    all_to_all x3, starting transfers between devices, spread(): return lax.all_to_all(copies, axis, split_axis=0, concat_axis=0, tiled=True)  26 us
    all_to_all x1, blocking collectives, layer(): lax.all_to_all(attended, 'seq', split_axis=0, concat_axis=1, tiled=True)  20.9 us
    all_gather x1, blocking collectives, layer(): merged_all = lax.all_gather(merged, 'rep', axis=0, tiled=True)  20.7 us
    dot_general x3, matrix products, merge_weights(): jnp.dot(both, attn_weight[:, part], preferred_element_type=jnp.float32)  4.62 us
    broadcast_in_dim x3, local copies, waits for them, and re-layouts, spread(): copies = jnp.broadcast_to(block[None], (lax.axis_size(axis),) + block.shape)  2.53 us
  transfers between devices with their start and end apart: 4, of which 2 were waited for; matrix products, arithmetic and copies ran while one was open for 8% of the time, Pallas kernels for 0%

profile of v2, /device:TPU:1, one launch (start us, length us, event | category | flops | bytes accessed | tf_op | source)
XLA Modules:
  0.0 116.4 jit_solution(7299836493731624031)
XLA Ops:
  0.0 0.0 copy-start
  0.0 1.1 copy.36
  1.1 1.3 %collective-permute-start = (bf16[64,512]{0,1:T(8,128)(2,1)S(1)}, bf16[64,512]{0,1:T(8,128)(2,1)S(1)}, u32[]{:S(2)}, u32[]{:S(2)}) collective-permute-start(bf16[64,512]{0,1:T(8,128)(2,1)S(1)} %slice.64), channel_id=1, source_target_pairs={{16,0},{32,16},{48,32},{64,48},{80,64},{96,80},{112,96},{128,112},... | collective-permute-start | bytes 196616 | tf_op jit(solution)/shard_map/ppermute | solution.py:18
  2.5 0.7 constant_dynamic-slice_fusion
  3.2 0.7 broadcast_in_dim.39
  3.8 0.8 broadcast_in_dim.40
  4.6 14.6 %all-to-all-start.1 = ((bf16[32,40,128]{2,1,0:T(8,128)(2,1)}), bf16[32,40,128]{2,1,0:T(8,128)(2,1)S(1)}, u32[]{:S(2)}, u32[]{:S(2)}) async-start(bf16[32,40,128]{2,1,0:T(8,128)(2,1)} %broadcast_in_dim.40), calls=%async_computation.1 | async-start | bytes 655360 | tf_op jit(solution)/shard_map/all_to_all | solution.py:69
  19.8 0.7 broadcast_subtract_fusion
  20.5 0.1 slice.49
  20.6 0.1 pad_add_fusion
  20.6 0.1 fusion.31
  20.7 0.2 convert_reduce_fusion
  20.9 0.0 collective-permute-done
  20.9 0.1 pad_maximum_fusion.1
  21.0 0.2 fusion.14
  21.2 0.0 copy-done
  21.3 0.3 fusion.6
  21.6 0.4 fusion.42
  21.9 0.2 fusion.13
  22.2 9.5 %all-to-all-done.1 = bf16[32,40,128]{2,1,0:T(8,128)(2,1)S(1)} async-done(((bf16[32,40,128]{2,1,0:T(8,128)(2,1)}), bf16[32,40,128]{2,1,0:T(8,128)(2,1)S(1)}, u32[]{:S(2)}, u32[]{:S(2)}) %all-to-all-start.1) | async-done | bytes 327712 | tf_op jit(solution)/shard_map/all_to_all | solution.py:69
  31.7 1.1 broadcast_in_dim.38
  32.8 4.8 %all-to-all-start = ((bf16[32,32,512]{2,1,0:T(8,128)(2,1)}), bf16[32,32,512]{2,1,0:T(8,128)(2,1)S(1)}, u32[]{:S(2)}, u32[]{:S(2)}) async-start(bf16[32,32,512]{2,1,0:T(8,128)(2,1)} %broadcast_in_dim.38), calls=%async_computation | async-start | bytes 2097152 | tf_op jit(solution)/shard_map/all_to_all | solution.py:69
  37.6 0.0 copy-start.1
  37.7 0.1 fusion.24
  37.8 1.5 %fusion.19 = f32[64,128]{1,0:T(8,128)S(1)} fusion(bf16[4096,3,128]{2,0,1:T(8,128)(2,1)} %param.13, bf16[32,4096]{1,0:T(8,128)(2,1)S(1)} %fusion.24, bf16[32,4096]{1,0:T(8,128)(2,1)S(1)} %bitcast_convert_fusion), kind=kOutput, calls=%fused_computation.29 | convolution fusion | flops 68157440 | bytes 1605632 | tf_op jit(solution)/shard_map/dot_general | solution.py:89
  39.3 1.5 %fusion.17 = f32[64,128]{1,0:T(8,128)S(1)} fusion(bf16[4096,3,128]{2,0,1:T(8,128)(2,1)} %param.13, bf16[32,4096]{1,0:T(8,128)(2,1)S(1)} %fusion.24, bf16[32,4096]{1,0:T(8,128)(2,1)S(1)} %bitcast_convert_fusion), kind=kOutput, calls=%fused_computation.27 | convolution fusion | flops 68157440 | bytes 1605632 | tf_op jit(solution)/shard_map/dot_general | solution.py:89
  40.9 1.5 %fusion.15 = f32[64,128]{1,0:T(8,128)S(1)} fusion(bf16[4096,3,128]{2,0,1:T(8,128)(2,1)} %param.13, bf16[32,4096]{1,0:T(8,128)(2,1)S(1)} %fusion.24, bf16[32,4096]{1,0:T(8,128)(2,1)S(1)} %bitcast_convert_fusion), kind=kOutput, calls=%fused_computation.25 | convolution fusion | flops 68157440 | bytes 1605632 | tf_op jit(solution)/shard_map/dot_general | solution.py:89
  42.4 20.9 %all-to-all-done = bf16[32,32,512]{2,1,0:T(8,128)(2,1)S(1)} async-done(((bf16[32,32,512]{2,1,0:T(8,128)(2,1)}), bf16[32,32,512]{2,1,0:T(8,128)(2,1)S(1)}, u32[]{:S(2)}, u32[]{:S(2)}) %all-to-all-start) | async-done | bytes 1048608 | tf_op jit(solution)/shard_map/all_to_all | solution.py:69
  63.3 0.0 copy-done.1
  63.3 0.5 fusion.5
  63.8 0.7 broadcast_in_dim.73
  64.5 6.7 %all-to-all-start.2 = ((f32[32,8,128]{2,1,0:T(8,128)}), f32[32,8,128]{2,1,0:T(8,128)S(1)}, u32[]{:S(2)}, u32[]{:S(2)}) async-start(f32[32,8,128]{2,1,0:T(8,128)} %broadcast_in_dim.73), calls=%async_computation.2 | async-start | bytes 262144 | tf_op jit(solution)/shard_map/all_to_all | solution.py:69
  71.1 20.7 %all_gather.3 = bf16[512,384]{1,0:T(8,128)(2,1)S(1)} all-gather(bf16[32,384]{1,0:T(8,128)(2,1)S(1)} %pad_maximum_fusion.5), channel_id=1, replica_groups=mesh['seq'=32,'rep'=16] {'rep'}, dimensions={0}, use_global_device_ids=true | all-gather | bytes 417792 | tf_op jit(solution)/shard_map/all_gather | solution.py:110
  91.9 0.0 all-to-all-done.2
  91.9 0.6 multiply_convert_fusion
  92.6 0.8 fusion.1
  93.3 0.5 fusion.2
  93.8 0.8 fusion.7
  94.6 0.2 copy.42
  94.7 20.9 %all_to_all.31 = bf16[32,32,128]{2,1,0:T(8,128)(2,1)S(1)} all-to-all(bf16[32,32,128]{2,1,0:T(8,128)(2,1)S(1)} %bitcast.82), channel_id=1, replica_groups=mesh['seq'=32,'rep'=16] {'seq'}, dimensions={0} | all-to-all | bytes 524288 | tf_op jit(solution)/shard_map/all_to_all | solution.py:123
  115.7 0.7 copy_bitcast_fusion
  (10 shorter events, 0.2 us)
Async XLA Ops:
  0.0 21.2 %copy-start = (bf16[512,512]{1,0:T(8,128)(2,1)S(1)}, bf16[512,512]{1,0:T(8,128)(2,1)}, u32[]{:S(2)}) copy-start(bf16[512,512]{1,0:T(8,128)(2,1)} %param.10) | copy-start | bytes 1572868
  1.1 19.8 %collective-permute-start = (bf16[64,512]{0,1:T(8,128)(2,1)S(1)}, bf16[64,512]{0,1:T(8,128)(2,1)S(1)}, u32[]{:S(2)}, u32[]{:S(2)}) collective-permute-start(bf16[64,512]{0,1:T(8,128)(2,1)S(1)} %slice.64), channel_id=1, source_target_pairs={{16,0},{32,16},{48,32},{64,48},{80,64},{96,80},{112,96},{128,112},... | collective-permute-start | bytes 196616 | tf_op jit(solution)/shard_map/ppermute | solution.py:18
  4.6 27.1 %all-to-all-start.1 = ((bf16[32,40,128]{2,1,0:T(8,128)(2,1)}), bf16[32,40,128]{2,1,0:T(8,128)(2,1)S(1)}, u32[]{:S(2)}, u32[]{:S(2)}) async-start(bf16[32,40,128]{2,1,0:T(8,128)(2,1)} %broadcast_in_dim.40), calls=%async_computation.1 | async-start | bytes 655360 | tf_op jit(solution)/shard_map/all_to_all | solution.py:69
  32.8 30.5 %all-to-all-start = ((bf16[32,32,512]{2,1,0:T(8,128)(2,1)}), bf16[32,32,512]{2,1,0:T(8,128)(2,1)S(1)}, u32[]{:S(2)}, u32[]{:S(2)}) async-start(bf16[32,32,512]{2,1,0:T(8,128)(2,1)} %broadcast_in_dim.38), calls=%async_computation | async-start | bytes 2097152 | tf_op jit(solution)/shard_map/all_to_all | solution.py:69
  37.6 25.7 %copy-start.1 = (bf16[512,128]{1,0:T(8,128)(2,1)S(1)}, bf16[512,128]{1,0:T(8,128)(2,1)}, u32[]{:S(2)}) copy-start(bf16[512,128]{1,0:T(8,128)(2,1)} %param.11) | copy-start | bytes 393220
  64.5 27.4 %all-to-all-start.2 = ((f32[32,8,128]{2,1,0:T(8,128)}), f32[32,8,128]{2,1,0:T(8,128)S(1)}, u32[]{:S(2)}, u32[]{:S(2)}) async-start(f32[32,8,128]{2,1,0:T(8,128)} %broadcast_in_dim.73), calls=%async_computation.2 | async-start | bytes 262144 | tf_op jit(solution)/shard_map/all_to_all | solution.py:69

commit v3 on v0

v3 whole, which is shorter than its diff:
```python
import functools

import jax
import jax.numpy as jnp
from jax import lax
from jax.experimental import pallas as pl
from jax.experimental.pallas import tpu as pltpu
from jax.sharding import PartitionSpec as P


HD = 128
LHD = 128
HALO = 64
ROWS = 32
GAIN_ROWS = 8
TILE = 256


epsilon = 1e-05


def shifted(shard, axis, by):
    size = lax.axis_size(axis)
    pairs = [(i, i + by) for i in range(size) if 0 <= i + by < size]
    return lax.ppermute(shard, axis, pairs)


def whole(count):
    return [pl.BlockSpec(memory_space=pltpu.VMEM)] * count


def scalars(count):
    return [pl.BlockSpec(memory_space=pltpu.SMEM)] * count


def rows_kernel(index_ref, weight_ref, gain_ref, out_ref):
    start = pl.multiple_of(index_ref[0] * ROWS, ROWS)
    rows = weight_ref[pl.ds(start, ROWS), :]
    gain = jnp.broadcast_to(gain_ref[...], (GAIN_ROWS, gain_ref.shape[1]))
    block = jnp.concatenate([rows, gain], axis=0)
    for target in range(out_ref.shape[0]):
        out_ref[target] = block


def weight_rows(out_weight, norm_gain, index, copies):
    return pl.pallas_call(
        rows_kernel,
        out_shape=jax.ShapeDtypeStruct((copies, ROWS + GAIN_ROWS, out_weight.shape[1]), jnp.bfloat16),
        in_specs=scalars(1) + whole(2),
        out_specs=pl.BlockSpec(memory_space=pltpu.VMEM),
        name="rows",
    )(index.reshape(1), out_weight, norm_gain.reshape(1, -1))


def keys_kernel(base_ref, starts_ref, straddle_ref, states_ref, weight_ref, keys_ref, first_ref, end_ref, states_out, weight_out):
    patches = first_ref.shape[0]
    shard_bytes = states_ref.shape[0]
    keys_ref[...] = jnp.dot(
        states_ref[...], weight_ref[...], preferred_element_type=jnp.float32
    ).astype(jnp.bfloat16)
    states_out[...] = states_ref[...]
    weight_out[...] = weight_ref[...]
    row = lax.broadcasted_iota(jnp.int32, first_ref.shape, 0)
    first = jnp.zeros(first_ref.shape, jnp.int32)
    end = jnp.zeros(first_ref.shape, jnp.int32)
    base = base_ref[0]
    for patch in range(patches):
        begin = starts_ref[patch] - base
        first = jnp.where(row == patch, begin, first)
        if patch > 0:
            end = jnp.where(row == patch - 1, begin, end)
    first_ref[...] = first
    end_ref[...] = jnp.where(row == patches - 1, shard_bytes + straddle_ref[0], end)


def own_keys(base, starts, straddle, states, key_weight):
    patches = starts.shape[0]
    bounds = jax.ShapeDtypeStruct((patches, 128), jnp.int32)
    return pl.pallas_call(
        keys_kernel,
        out_shape=(
            jax.ShapeDtypeStruct(states.shape, jnp.bfloat16),
            bounds,
            bounds,
            jax.ShapeDtypeStruct(states.shape, jnp.bfloat16),
            jax.ShapeDtypeStruct(key_weight.shape, jnp.bfloat16),
        ),
        in_specs=scalars(3) + whole(2),
        out_specs=tuple(whole(5)),
        compiler_params=pltpu.CompilerParams(vmem_limit_bytes=8 << 20),
        name="own_keys",
    )(base.reshape(1), starts, straddle, states, key_weight)


def pool_kernel(first_ref, end_ref, states_ref, halo_ref, keys_ref, weight_ref, out_ref):
    window = jnp.concatenate([states_ref[...], halo_ref[...]], axis=0)
    halo_keys = jnp.dot(
        halo_ref[...], weight_ref[...], preferred_element_type=jnp.float32
    ).astype(jnp.bfloat16)
    keys = jnp.concatenate([keys_ref[...], halo_keys], axis=0)
    patches = first_ref.shape[0]
    position = lax.broadcasted_iota(jnp.int32, (patches, window.shape[0]), 1)
    member = (position >= first_ref[:, :1]) & (position < end_ref[:, :1])
    ones = jnp.where(member, jnp.float32(1.0), jnp.float32(0.0))
    byte_count = jnp.sum(ones, axis=1, keepdims=True)
    query = (
        jnp.dot(ones.astype(jnp.bfloat16), window, preferred_element_type=jnp.float32) / byte_count
    ).astype(jnp.bfloat16)
    pooled = []
    for head in range(window.shape[1] // LHD):
        part = slice(head * LHD, (head + 1) * LHD)
        scores = lax.dot_general(
            query[:, part],
            keys[:, part],
            (((1,), (1,)), ((), ())),
            preferred_element_type=jnp.float32,
        ) * jnp.float32(LHD**-0.5)
        scores = jnp.where(member, scores, jnp.float32(-1e30))
        row_peak = jnp.max(scores, axis=1, keepdims=True)
        expo = jnp.where(member, jnp.exp(scores - row_peak), jnp.float32(0.0))
        cross = (expo / jnp.sum(expo, axis=1, keepdims=True)).astype(jnp.bfloat16)
        pooled.append(
            jnp.dot(cross, window[:, part], preferred_element_type=jnp.float32).astype(jnp.bfloat16)
        )
    block = jnp.concatenate(pooled, axis=1)
    for target in range(out_ref.shape[0]):
        out_ref[target] = block


def pool(first, end, states, halo, keys, key_weight, copies):
    patches, width = first.shape[0], states.shape[1]
    return pl.pallas_call(
        pool_kernel,
        out_shape=jax.ShapeDtypeStruct((copies, patches, width), jnp.bfloat16),
        in_specs=whole(6),
        out_specs=pl.BlockSpec(memory_space=pltpu.VMEM),
        compiler_params=pltpu.CompilerParams(vmem_limit_bytes=16 << 20),
        name="pool",
    )(first, end, states, halo, keys, key_weight)


def merge_kernel(blocks_ref, weight_ref, out_ref, total_ref):
    step = pl.program_id(0)

    @pl.when(step == 0)
    def _():
        total_ref[...] = jnp.zeros_like(total_ref)

    high, low = [], []
    for shard in range(blocks_ref.shape[0]):
        gain = blocks_ref[shard, ROWS:, :].astype(jnp.float32)[:1]
        scaled = blocks_ref[shard, :ROWS, :].astype(jnp.float32) * gain
        top = scaled.astype(jnp.bfloat16)
        high.append(top)
        low.append((scaled - top.astype(jnp.float32)).astype(jnp.bfloat16))
    both = jnp.concatenate(
        [jnp.concatenate(high, axis=1), jnp.concatenate(low, axis=1)], axis=0
    )
    for part in range(weight_ref.shape[0]):
        total_ref[:, part * HD : (part + 1) * HD] += jnp.dot(
            both, weight_ref[part], preferred_element_type=jnp.float32
        )

    @pl.when(step == pl.num_programs(0) - 1)
    def _():
        out_ref[...] = (total_ref[:ROWS] + total_ref[ROWS:]).astype(jnp.bfloat16)


def merge_weights(blocks, attn_weight):
    shards_total, block_rows, columns = blocks.shape
    steps = 4
    group = shards_total // steps
    planes = jnp.swapaxes(attn_weight, 0, 1)
    parts, _, width = planes.shape
    return pl.pallas_call(
        merge_kernel,
        out_shape=jax.ShapeDtypeStruct((ROWS, parts * width), jnp.bfloat16),
        grid=(steps,),
        in_specs=[
            pl.BlockSpec((group, block_rows, columns), lambda s: (s, 0, 0)),
            pl.BlockSpec((parts, group * columns, width), lambda s: (0, s, 0)),
        ],
        out_specs=pl.BlockSpec((ROWS, parts * width), lambda s: (0, 0)),
        scratch_shapes=[pltpu.VMEM((2 * ROWS, parts * width), jnp.float32)],
        compiler_params=pltpu.CompilerParams(vmem_limit_bytes=16 << 20),
        name="merge",
    )(blocks, planes)


def attend_kernel(model_width, square_ref, pooled_ref, merged_ref, out_ref, view_ref):
    square = jnp.sum(square_ref[...], axis=0) / jnp.float32(model_width)
    inverse = lax.rsqrt(square + jnp.float32(epsilon))
    diagonal = lax.broadcasted_iota(jnp.int32, (128, 128), 0) == lax.broadcasted_iota(
        jnp.int32, (128, 128), 1
    )
    patches = pooled_ref.shape[0]
    for tile in range(patches // 128):
        rows = slice(tile * 128, (tile + 1) * 128)
        spread_row = jnp.broadcast_to(inverse[tile : tile + 1, :], (128, 128))
        column = jnp.sum(
            jnp.where(diagonal, spread_row, jnp.float32(0.0)), axis=1, keepdims=True
        )
        view_ref[rows, :] = (
            jnp.dot(pooled_ref[rows, :], merged_ref[...], preferred_element_type=jnp.float32)
            * column
        ).astype(jnp.bfloat16)
    for tile in range(patches // TILE):
        rows = slice(tile * TILE, (tile + 1) * TILE)
        seen = (tile + 1) * TILE
        scores = lax.dot_general(
            view_ref[rows, :HD],
            view_ref[:seen, HD : 2 * HD],
            (((1,), (1,)), ((), ())),
            preferred_element_type=jnp.float32,
        ) * jnp.float32(HD**-0.5)
        causal = lax.broadcasted_iota(jnp.int32, (TILE, seen), 0) + tile * TILE >= (
            lax.broadcasted_iota(jnp.int32, (TILE, seen), 1)
        )
        scores = jnp.where(causal, scores, jnp.float32(-1e30))
        row_peak = jnp.max(scores, axis=1, keepdims=True)
        expo = jnp.exp(scores - row_peak)
        probs = (expo * (jnp.float32(1.0) / jnp.sum(expo, axis=1, keepdims=True))).astype(
            jnp.bfloat16
        )
        out_ref[rows, :] = jnp.dot(
            probs, view_ref[:seen, 2 * HD :], preferred_element_type=jnp.float32
        ).astype(jnp.bfloat16)


def attend(model_width, square_all, pooled_all, merged_all):
    patches = pooled_all.shape[0]
    return pl.pallas_call(
        functools.partial(attend_kernel, model_width),
        out_shape=jax.ShapeDtypeStruct((patches, HD), jnp.bfloat16),
        in_specs=whole(3),
        out_specs=pl.BlockSpec(memory_space=pltpu.VMEM),
        scratch_shapes=[pltpu.VMEM((patches, merged_all.shape[1]), jnp.bfloat16)],
        compiler_params=pltpu.CompilerParams(vmem_limit_bytes=24 << 20),
        name="attend",
    )(square_all, pooled_all, merged_all)


def exchange(blocks, axis):
    return lax.all_to_all(blocks, axis, split_axis=0, concat_axis=0, tiled=True)


def layer(states, starts, straddle, key_weight, out_weight, norm_gain, attn_weight):
    seq = lax.axis_size("seq")
    base = lax.axis_index("seq") * states.shape[0]
    model_width = attn_weight.shape[0]
    pooled_width = out_weight.shape[0]

    weight_blocks = exchange(weight_rows(out_weight, norm_gain, lax.axis_index("rep"), seq), "seq")
    halo_rows = shifted(states[:HALO], "seq", -1)
    keys, first, end, own, weight = own_keys(base, starts, straddle, states, key_weight)
    pooled_blocks = pool(first, end, own, halo_rows, keys, weight, seq)
    pooled_all = exchange(pooled_blocks, "seq").reshape(-1, pooled_width)
    merged = merge_weights(weight_blocks, attn_weight)
    merged_all = lax.all_gather(merged, "rep", axis=0, tiled=True)
    part = lax.dot_general(
        out_weight, pooled_all, (((0,), (1,)), ((), ())), preferred_element_type=jnp.float32
    )
    part_square = jnp.sum(part * part, axis=0).reshape(-1, 128)
    square_all = exchange(jnp.broadcast_to(part_square[None], (seq,) + part_square.shape), "seq")
    attended = attend(model_width, square_all, pooled_all, merged_all)
    return lax.all_to_all(attended, "seq", split_axis=0, concat_axis=1, tiled=True)


def solution(mesh):
    placed = (
        P(("rep", "seq"), None),
        P(("rep", "seq")),
        P(("rep", "seq")),
        P(),
        P(None, "seq"),
        P("seq"),
        P(None, None, "seq"),
    )
    return jax.shard_map(
        layer, mesh=mesh, in_specs=placed, out_specs=P(("rep", "seq"), None), check_vma=False
    )
```

time: 248 us -> 123 us (0.50)
  waiting for transfers between devices: 151 us -> 34.1 us
  starting transfers between devices: 1.33 us -> 28.3 us
  blocking collectives: 56.2 us -> 42.5 us
  between operations: 14.2 us -> 0.75 us
  matrix products: 13.4 us -> 0.49 us
  Pallas kernels: 0 us -> 9.29 us
    all_gather x2 -> x0, waiting for transfers between devices: 150 us -> none  [the longest x1 102 us: shards(): lax.all_gather(normed, 'seq', axis=0, tiled=True)]
    all_to_all x0 -> x3, waiting for transfers between devices: none -> 33.9 us  [exchange(): return lax.all_to_all(blocks, axis, split_axis=0, concat_axis=0, tiled=True)]
    all_to_all x0 -> x3, starting transfers between devices: none -> 27.1 us  [exchange(): return lax.all_to_all(blocks, axis, split_axis=0, concat_axis=0, tiled=True)]
    all_gather x1, blocking collectives: 40.8 us -> 21.6 us  [layer(): merged_all = lax.all_gather(merged, 'rep', axis=0, tiled=True)]
    dot_general x7 -> x1, matrix products: 13.1 us -> 0.49 us  [layer(): lax.dot_general(out_weight, pooled_all, (((0,), (1,)), ((), ())), preferr...]
    pallas_call x0 -> x5, Pallas kernels: none -> 9.29 us  [the longest x1 2.78 us: attend(): pl.pallas_call(functools.partial(attend_kernel, model_width), out_shape=j...]
    all_to_all x1, blocking collectives: 15.4 us -> 20.9 us  [layer(): lax.all_to_all(attended, 'seq', split_axis=0, concat_axis=1, tiled=True)]
    unnamed x4 -> x10, local copies, waits for them, and re-layouts: 5.78 us -> 4.51 us
  transfers between devices with their start and end apart: 3 -> 4, of which waited for: 2 -> 3; matrix products, arithmetic and copies ran while one was open for 3% -> 0% of each run, Pallas kernels for 0% -> 3%
where the time goes in v3:
time: 123 us; the launch traced here: 122 us
  blocking collectives  42.5 us (35%)
  waiting for transfers between devices  34.1 us (28%)
  starting transfers between devices  28.3 us (23%)
  Pallas kernels  9.29 us (8%)
  local copies, waits for them, and re-layouts  6.77 us (6%)
    all_to_all x3, waiting for transfers between devices, exchange(): return lax.all_to_all(blocks, axis, split_axis=0, concat_axis=0, tiled=True)  33.9 us
    all_to_all x3, starting transfers between devices, exchange(): return lax.all_to_all(blocks, axis, split_axis=0, concat_axis=0, tiled=True)  27.1 us
    all_gather x1, blocking collectives, layer(): merged_all = lax.all_gather(merged, 'rep', axis=0, tiled=True)  21.6 us
    all_to_all x1, blocking collectives, layer(): lax.all_to_all(attended, 'seq', split_axis=0, concat_axis=1, tiled=True)  20.9 us
    unnamed x10, local copies, waits for them, and re-layouts  4.51 us
    pallas_call x1, Pallas kernels, attend(): pl.pallas_call(functools.partial(attend_kernel, model_width), out_shape=j...  2.78 us
    pallas_call x1, Pallas kernels, pool(): pl.pallas_call(pool_kernel, out_shape=jax.ShapeDtypeStruct((copies, patch...  2.66 us
  transfers between devices with their start and end apart: 4, of which 3 were waited for; matrix products, arithmetic and copies ran while one was open for 0% of the time, Pallas kernels for 3%

profile of v3, /device:TPU:1, one launch (start us, length us, event | category | flops | bytes accessed | tf_op | source)
XLA Modules:
  0.0 122.3 jit_solution(13409309047316984492)
XLA Ops:
  0.0 0.0 copy-start.4
  0.0 0.9 slice.3
  0.9 1.3 %collective-permute-start = (bf16[64,512]{1,0:T(8,128)(2,1)S(1)}, bf16[64,512]{1,0:T(8,128)(2,1)S(1)}, u32[]{:S(2)}, u32[]{:S(2)}) collective-permute-start(bf16[64,512]{1,0:T(8,128)(2,1)S(1)} %slice.3), channel_id=1, source_target_pairs={{16,0},{32,16},{48,32},{64,48},{80,64},{96,80},{112,96},{128,112},... | collective-permute-start | bytes 196616 | tf_op jit(solution)/shard_map/ppermute | solution.py:25
  2.8 0.0 copy-start.1
  2.8 1.0 copy-done.1
  3.9 0.0 copy-start.2
  3.9 0.9 copy-done.2
  4.8 0.0 copy-start.3
  4.8 0.7 copy-done.3
  5.5 0.8 own_keys.1
  6.3 0.2 collective-permute-done.halo_ref
  6.5 2.7 %pool.1 = bf16[32,32,512]{2,1,0:T(8,128)(2,1)} custom-call(s32[32,128]{1,0:T(8,128)S(1)} %get-tuple-element.10.first_ref, s32[32,128]{1,0:T(8,128)S(1)} %get-tuple-element.11.end_ref, bf16[192,512]{1,0:T(8,128)(2,1)S(1)} %get-tuple-element.12.states_ref, bf16[64,512]{1,0:T(8,128)(2,1)S(1)} %collective-permute-done.halo_ref, ...), custom_call_target="tpu_custom_call" | custom-call | tf_op jit(solution)/shard_map/pool/pallas_call | solution.py:132
  9.1 15.0 %all-to-all-start = ((bf16[32,32,512]{2,1,0:T(8,128)(2,1)}), bf16[32,32,512]{2,1,0:T(8,128)(2,1)S(1)}, u32[]{:S(2)}, u32[]{:S(2)}) async-start(bf16[32,32,512]{2,1,0:T(8,128)(2,1)} %pool.1), calls=%async_computation | async-start | bytes 2097152 | tf_op jit(solution)/shard_map/all_to_all | solution.py:244
  24.1 1.7 %rows.1 = bf16[32,40,128]{2,1,0:T(8,128)(2,1)} custom-call(s32[1]{0:T(128)} %bitcast.3.index_ref, bf16[512,128]{1,0:T(8,128)(2,1)} %weight_ref.3, bf16[1,128]{1,0:T(2,128)(2,1)} %bitcast.20), custom_call_target="tpu_custom_call" | custom-call | tf_op jit(solution)/shard_map/rows/pallas_call | solution.py:46
  25.8 23.6 %all-to-all-done = bf16[32,32,512]{2,1,0:T(8,128)(2,1)S(1)} async-done(((bf16[32,32,512]{2,1,0:T(8,128)(2,1)}), bf16[32,32,512]{2,1,0:T(8,128)(2,1)S(1)}, u32[]{:S(2)}, u32[]{:S(2)}) %all-to-all-start) | async-done | bytes 1048608 | tf_op jit(solution)/shard_map/all_to_all | solution.py:244
  49.4 6.8 %all-to-all-start.2 = ((bf16[32,40,128]{2,1,0:T(8,128)(2,1)}), bf16[32,40,128]{2,1,0:T(8,128)(2,1)S(1)}, u32[]{:S(2)}, u32[]{:S(2)}) async-start(bf16[32,40,128]{2,1,0:T(8,128)(2,1)} %rows.1), calls=%async_computation.2 | async-start | bytes 655360 | tf_op jit(solution)/shard_map/all_to_all | solution.py:244
  56.2 0.0 copy-done.4
  56.2 0.5 fusion
  56.7 10.3 %all-to-all-done.2.blocks_ref = bf16[32,40,128]{2,1,0:T(8,128)(2,1)S(1)} async-done(((bf16[32,40,128]{2,1,0:T(8,128)(2,1)}), bf16[32,40,128]{2,1,0:T(8,128)(2,1)S(1)}, u32[]{:S(2)}, u32[]{:S(2)}) %all-to-all-start.2) | async-done | bytes 327712 | tf_op jit(solution)/shard_map/all_to_all | solution.py:244
  67.0 0.7 broadcast_in_dim.8
  67.7 5.3 %all-to-all-start.1 = ((f32[32,8,128]{2,1,0:T(8,128)}), f32[32,8,128]{2,1,0:T(8,128)S(1)}, u32[]{:S(2)}, u32[]{:S(2)}) async-start(f32[32,8,128]{2,1,0:T(8,128)} %broadcast_in_dim.8), calls=%async_computation.1 | async-start | bytes 262144 | tf_op jit(solution)/shard_map/all_to_all | solution.py:244
  73.0 0.0 copy-start
  73.0 1.9 %copy-done = bf16[4096,3,128]{2,0,1:T(8,128)(2,1)S(1)} copy-done((bf16[4096,3,128]{2,0,1:T(8,128)(2,1)S(1)}, bf16[4096,3,128]{2,0,1:T(8,128)(2,1)}, u32[]{:S(2)}) %copy-start) | copy-done | bytes 3145752
  74.9 1.3 %merge.1 = bf16[32,384]{1,0:T(8,128)(2,1)S(1)} custom-call(bf16[32,40,128]{2,1,0:T(8,128)(2,1)S(1)} %all-to-all-done.2.blocks_ref, bf16[3,4096,128]{2,1,0:T(8,128)(2,1)S(1)} %bitcast.17), custom_call_target="tpu_custom_call" | custom-call | tf_op jit(solution)/shard_map/merge/pallas_call | solution.py:175
  76.2 21.6 %all_gather.3.merged_ref = bf16[512,384]{1,0:T(8,128)(2,1)S(1)} all-gather(bf16[32,384]{1,0:T(8,128)(2,1)S(1)} %merge.1), channel_id=1, replica_groups=mesh['seq'=32,'rep'=16] {'rep'}, dimensions={0}, use_global_device_ids=true | all-gather | bytes 417792 | tf_op jit(solution)/shard_map/all_gather | solution.py:259
  97.8 0.0 all-to-all-done.1.square_ref
  97.8 2.8 %attend.1 = bf16[1024,128]{1,0:T(8,128)(2,1)S(1)} custom-call(f32[32,8,128]{2,1,0:T(8,128)S(1)} %all-to-all-done.1.square_ref, bf16[1024,512]{1,0:T(8,128)(2,1)S(1)} %bitcast.16, bf16[512,384]{1,0:T(8,128)(2,1)S(1)} %all_gather.3.merged_ref), custom_call_target="tpu_custom_call" | custom-call | tf_op jit(solution)/shard_map/attend/pallas_call | solution.py:232
  100.6 20.9 %all_to_all.34 = bf16[32,32,128]{2,1,0:T(8,128)(2,1)S(1)} all-to-all(bf16[32,32,128]{2,1,0:T(8,128)(2,1)S(1)} %bitcast.18), channel_id=1, replica_groups=mesh['seq'=32,'rep'=16] {'seq'}, dimensions={0} | all-to-all | bytes 524288 | tf_op jit(solution)/shard_map/all_to_all | solution.py:266
  121.5 0.7 copy_bitcast_fusion
Async XLA Ops:
  0.0 56.2 %copy-start.4 = (bf16[512,128]{1,0:T(8,128)(2,1)S(1)}, bf16[512,128]{1,0:T(8,128)(2,1)}, u32[]{:S(2)}) copy-start(bf16[512,128]{1,0:T(8,128)(2,1)} %weight_ref.3) | copy-start | bytes 393220
  0.9 5.6 %collective-permute-start = (bf16[64,512]{1,0:T(8,128)(2,1)S(1)}, bf16[64,512]{1,0:T(8,128)(2,1)S(1)}, u32[]{:S(2)}, u32[]{:S(2)}) collective-permute-start(bf16[64,512]{1,0:T(8,128)(2,1)S(1)} %slice.3), channel_id=1, source_target_pairs={{16,0},{32,16},{48,32},{64,48},{80,64},{96,80},{112,96},{128,112},... | collective-permute-start | bytes 196616 | tf_op jit(solution)/shard_map/ppermute | solution.py:25
  2.8 1.0 copy-start.1
  3.9 0.9 copy-start.2
  4.8 0.7 copy-start.3
  9.1 40.2 %all-to-all-start = ((bf16[32,32,512]{2,1,0:T(8,128)(2,1)}), bf16[32,32,512]{2,1,0:T(8,128)(2,1)S(1)}, u32[]{:S(2)}, u32[]{:S(2)}) async-start(bf16[32,32,512]{2,1,0:T(8,128)(2,1)} %pool.1), calls=%async_computation | async-start | bytes 2097152 | tf_op jit(solution)/shard_map/all_to_all | solution.py:244
  49.4 17.7 %all-to-all-start.2 = ((bf16[32,40,128]{2,1,0:T(8,128)(2,1)}), bf16[32,40,128]{2,1,0:T(8,128)(2,1)S(1)}, u32[]{:S(2)}, u32[]{:S(2)}) async-start(bf16[32,40,128]{2,1,0:T(8,128)(2,1)} %rows.1), calls=%async_computation.2 | async-start | bytes 655360 | tf_op jit(solution)/shard_map/all_to_all | solution.py:244
  67.7 30.1 %all-to-all-start.1 = ((f32[32,8,128]{2,1,0:T(8,128)}), f32[32,8,128]{2,1,0:T(8,128)S(1)}, u32[]{:S(2)}, u32[]{:S(2)}) async-start(f32[32,8,128]{2,1,0:T(8,128)} %broadcast_in_dim.8), calls=%async_computation.1 | async-start | bytes 262144 | tf_op jit(solution)/shard_map/all_to_all | solution.py:244
  73.0 1.9 %copy-start = (bf16[4096,3,128]{2,0,1:T(8,128)(2,1)S(1)}, bf16[4096,3,128]{2,0,1:T(8,128)(2,1)}, u32[]{:S(2)}) copy-start(bf16[4096,3,128]{2,0,1:T(8,128)(2,1)} %param.13) | copy-start | bytes 9437188

commit v4 on v3

--- a/solution.py
+++ b/solution.py
@@ -12,8 +12,8 @@
 LHD = 128
 HALO = 64
 ROWS = 32
-GAIN_ROWS = 8
 TILE = 256
+WIDE = 512
 
 
 epsilon = 1e-05
@@ -33,33 +33,21 @@
     return [pl.BlockSpec(memory_space=pltpu.SMEM)] * count
 
 
-def rows_kernel(index_ref, weight_ref, gain_ref, out_ref):
+def prepare_kernel(
+    index_ref, base_ref, starts_ref, straddle_ref, out_weight_ref, gain_ref, states_ref, weight_ref,
+    blocks_ref, halo_ref, keys_ref, first_ref, end_ref, own_ref, own_weight_ref,
+    rows_ref, columns_ref, sems,
+):
     start = pl.multiple_of(index_ref[0] * ROWS, ROWS)
-    rows = weight_ref[pl.ds(start, ROWS), :]
-    gain = jnp.broadcast_to(gain_ref[...], (GAIN_ROWS, gain_ref.shape[1]))
-    block = jnp.concatenate([rows, gain], axis=0)
-    for target in range(out_ref.shape[0]):
-        out_ref[target] = block
-
-
-def weight_rows(out_weight, norm_gain, index, copies):
-    return pl.pallas_call(
-        rows_kernel,
-        out_shape=jax.ShapeDtypeStruct((copies, ROWS + GAIN_ROWS, out_weight.shape[1]), jnp.bfloat16),
-        in_specs=scalars(1) + whole(2),
-        out_specs=pl.BlockSpec(memory_space=pltpu.VMEM),
-        name="rows",
-    )(index.reshape(1), out_weight, norm_gain.reshape(1, -1))
-
-
-def keys_kernel(base_ref, starts_ref, straddle_ref, states_ref, weight_ref, keys_ref, first_ref, end_ref, states_out, weight_out):
+    copies = [
+        pltpu.make_async_copy(out_weight_ref.at[pl.ds(start, ROWS), :], rows_ref, sems.at[0]),
+        pltpu.make_async_copy(gain_ref, columns_ref, sems.at[1]),
+        pltpu.make_async_copy(states_ref, own_ref, sems.at[2]),
+        pltpu.make_async_copy(weight_ref, own_weight_ref, sems.at[3]),
+    ]
+    for copy in copies:
+        copy.start()
     patches = first_ref.shape[0]
-    shard_bytes = states_ref.shape[0]
-    keys_ref[...] = jnp.dot(
-        states_ref[...], weight_ref[...], preferred_element_type=jnp.float32
-    ).astype(jnp.bfloat16)
-    states_out[...] = states_ref[...]
-    weight_out[...] = weight_ref[...]
     row = lax.broadcasted_iota(jnp.int32, first_ref.shape, 0)
     first = jnp.zeros(first_ref.shape, jnp.int32)
     end = jnp.zeros(first_ref.shape, jnp.int32)
@@ -70,26 +58,49 @@
         if patch > 0:
             end = jnp.where(row == patch - 1, begin, end)
     first_ref[...] = first
-    end_ref[...] = jnp.where(row == patches - 1, shard_bytes + straddle_ref[0], end)
-
-
-def own_keys(base, starts, straddle, states, key_weight):
-    patches = starts.shape[0]
+    end_ref[...] = jnp.where(row == patches - 1, own_ref.shape[0] + straddle_ref[0], end)
+    copies[0].wait()
+    copies[1].wait()
+    block = (
+        rows_ref[...].astype(jnp.float32) * columns_ref[...].astype(jnp.float32)
+    ).astype(jnp.bfloat16)
+    for target in range(blocks_ref.shape[0]):
+        blocks_ref[target] = block
+    copies[2].wait()
+    halo_ref[...] = own_ref[:HALO, :]
+    copies[3].wait()
+    keys_ref[...] = jnp.dot(
+        own_ref[...], own_weight_ref[...], preferred_element_type=jnp.float32
+    ).astype(jnp.bfloat16)
+
+
+def prepare(index, base, starts, straddle, out_weight, norm_gain, states, key_weight, copies):
+    patches, width = starts.shape[0], states.shape[1]
+    columns = out_weight.shape[1]
     bounds = jax.ShapeDtypeStruct((patches, 128), jnp.int32)
     return pl.pallas_call(
-        keys_kernel,
+        prepare_kernel,
         out_shape=(
+            jax.ShapeDtypeStruct((copies, ROWS, columns), jnp.bfloat16),
+            jax.ShapeDtypeStruct((HALO, width), jnp.bfloat16),
             jax.ShapeDtypeStruct(states.shape, jnp.bfloat16),
             bounds,
             bounds,
             jax.ShapeDtypeStruct(states.shape, jnp.bfloat16),
             jax.ShapeDtypeStruct(key_weight.shape, jnp.bfloat16),
         ),
-        in_specs=scalars(3) + whole(2),
-        out_specs=tuple(whole(5)),
-        compiler_params=pltpu.CompilerParams(vmem_limit_bytes=8 << 20),
-        name="own_keys",
-    )(base.reshape(1), starts, straddle, states, key_weight)
+        in_specs=scalars(4) + [pl.BlockSpec(memory_space=pltpu.HBM)] * 4,
+        out_specs=tuple(whole(7)),
+        scratch_shapes=[
+            pltpu.VMEM((ROWS, columns), jnp.bfloat16),
+            pltpu.VMEM((1, columns), jnp.bfloat16),
+            pltpu.SemaphoreType.DMA((4,)),
+        ],
+        name="prepare",
+    )(
+        index.reshape(1), base.reshape(1), starts, straddle,
+        out_weight, norm_gain.reshape(1, -1), states, key_weight,
+    )
 
 
 def pool_kernel(first_ref, end_ref, states_ref, halo_ref, keys_ref, weight_ref, out_ref):
@@ -134,7 +145,6 @@
         out_shape=jax.ShapeDtypeStruct((copies, patches, width), jnp.bfloat16),
         in_specs=whole(6),
         out_specs=pl.BlockSpec(memory_space=pltpu.VMEM),
-        compiler_params=pltpu.CompilerParams(vmem_limit_bytes=16 << 20),
         name="pool",
     )(first, end, states, halo, keys, key_weight)
 
@@ -146,24 +156,15 @@
     def _():
         total_ref[...] = jnp.zeros_like(total_ref)
 
-    high, low = [], []
-    for shard in range(blocks_ref.shape[0]):
-        gain = blocks_ref[shard, ROWS:, :].astype(jnp.float32)[:1]
-        scaled = blocks_ref[shard, :ROWS, :].astype(jnp.float32) * gain
-        top = scaled.astype(jnp.bfloat16)
-        high.append(top)
-        low.append((scaled - top.astype(jnp.float32)).astype(jnp.bfloat16))
-    both = jnp.concatenate(
-        [jnp.concatenate(high, axis=1), jnp.concatenate(low, axis=1)], axis=0
-    )
+    rows = jnp.concatenate([blocks_ref[shard] for shard in range(blocks_ref.shape[0])], axis=1)
     for part in range(weight_ref.shape[0]):
         total_ref[:, part * HD : (part + 1) * HD] += jnp.dot(
-            both, weight_ref[part], preferred_element_type=jnp.float32
+            rows, weight_ref[part], preferred_element_type=jnp.float32
         )
 
     @pl.when(step == pl.num_programs(0) - 1)
     def _():
-        out_ref[...] = (total_ref[:ROWS] + total_ref[ROWS:]).astype(jnp.bfloat16)
+        out_ref[...] = total_ref[...].astype(jnp.bfloat16)
 
 
 def merge_weights(blocks, attn_weight):
@@ -181,7 +182,7 @@
             pl.BlockSpec((parts, group * columns, width), lambda s: (0, s, 0)),
         ],
         out_specs=pl.BlockSpec((ROWS, parts * width), lambda s: (0, 0)),
-        scratch_shapes=[pltpu.VMEM((2 * ROWS, parts * width), jnp.float32)],
+        scratch_shapes=[pltpu.VMEM((ROWS, parts * width), jnp.float32)],
         compiler_params=pltpu.CompilerParams(vmem_limit_bytes=16 << 20),
         name="merge",
     )(blocks, planes)
@@ -194,37 +195,51 @@
         jnp.int32, (128, 128), 1
     )
     patches = pooled_ref.shape[0]
+    columns = []
     for tile in range(patches // 128):
-        rows = slice(tile * 128, (tile + 1) * 128)
         spread_row = jnp.broadcast_to(inverse[tile : tile + 1, :], (128, 128))
-        column = jnp.sum(
-            jnp.where(diagonal, spread_row, jnp.float32(0.0)), axis=1, keepdims=True
-        )
+        columns.append(
+            jnp.sum(jnp.where(diagonal, spread_row, jnp.float32(0.0)), axis=1, keepdims=True)
+        )
+    for tile in range(patches // WIDE):
+        rows = slice(tile * WIDE, (tile + 1) * WIDE)
+        column = jnp.concatenate(columns[tile * WIDE // 128 : (tile + 1) * WIDE // 128], axis=0)
         view_ref[rows, :] = (
             jnp.dot(pooled_ref[rows, :], merged_ref[...], preferred_element_type=jnp.float32)
             * column
         ).astype(jnp.bfloat16)
+    causal = lax.broadcasted_iota(jnp.int32, (TILE, TILE), 0) >= lax.broadcasted_iota(
+        jnp.int32, (TILE, TILE), 1
+    )
+    scale = jnp.float32(HD**-0.5)
     for tile in range(patches // TILE):
         rows = slice(tile * TILE, (tile + 1) * TILE)
-        seen = (tile + 1) * TILE
-        scores = lax.dot_general(
-            view_ref[rows, :HD],
-            view_ref[:seen, HD : 2 * HD],
-            (((1,), (1,)), ((), ())),
-            preferred_element_type=jnp.float32,
-        ) * jnp.float32(HD**-0.5)
-        causal = lax.broadcasted_iota(jnp.int32, (TILE, seen), 0) + tile * TILE >= (
-            lax.broadcasted_iota(jnp.int32, (TILE, seen), 1)
-        )
-        scores = jnp.where(causal, scores, jnp.float32(-1e30))
-        row_peak = jnp.max(scores, axis=1, keepdims=True)
-        expo = jnp.exp(scores - row_peak)
-        probs = (expo * (jnp.float32(1.0) / jnp.sum(expo, axis=1, keepdims=True))).astype(
-            jnp.bfloat16
-        )
-        out_ref[rows, :] = jnp.dot(
-            probs, view_ref[:seen, 2 * HD :], preferred_element_type=jnp.float32
-        ).astype(jnp.bfloat16)
+        query = view_ref[rows, :HD]
+
+        def against(keys):
+            return lax.dot_general(
+                query, keys, (((1,), (1,)), ((), ())), preferred_element_type=jnp.float32
+            )
+
+        near = jnp.where(causal, against(view_ref[rows, HD : 2 * HD]), jnp.float32(-1e30))
+        peak = jnp.max(near, axis=1, keepdims=True)
+        if tile > 0:
+            far = against(view_ref[: tile * TILE, HD : 2 * HD])
+            peak = jnp.maximum(peak, jnp.max(far, axis=1, keepdims=True))
+        near = jnp.exp((near - peak) * scale)
+        total = jnp.sum(near, axis=1, keepdims=True)
+        result = jnp.dot(
+            near.astype(jnp.bfloat16), view_ref[rows, 2 * HD :], preferred_element_type=jnp.float32
+        )
+        if tile > 0:
+            far = jnp.exp((far - peak) * scale)
+            total = total + jnp.sum(far, axis=1, keepdims=True)
+            result = result + jnp.dot(
+                far.astype(jnp.bfloat16),
+                view_ref[: tile * TILE, 2 * HD :],
+                preferred_element_type=jnp.float32,
+            )
+        out_ref[rows, :] = (result * (jnp.float32(1.0) / total)).astype(jnp.bfloat16)
 
 
 def attend(model_width, square_all, pooled_all, merged_all):
@@ -250,9 +265,12 @@
     model_width = attn_weight.shape[0]
     pooled_width = out_weight.shape[0]
 
-    weight_blocks = exchange(weight_rows(out_weight, norm_gain, lax.axis_index("rep"), seq), "seq")
-    halo_rows = shifted(states[:HALO], "seq", -1)
-    keys, first, end, own, weight = own_keys(base, starts, straddle, states, key_weight)
+    row_blocks, edge, keys, first, end, own, weight = prepare(
+        lax.axis_index("rep"), base, starts, straddle,
+        out_weight, norm_gain, states, key_weight, seq,
+    )
+    weight_blocks = exchange(row_blocks, "seq")
+    halo_rows = shifted(edge, "seq", -1)
     pooled_blocks = pool(first, end, own, halo_rows, keys, weight, seq)
     pooled_all = exchange(pooled_blocks, "seq").reshape(-1, pooled_width)
     merged = merge_weights(weight_blocks, attn_weight)

time: 123 us -> 126 us (1.024)
  blocking collectives: 42.5 us -> 83.5 us
  waiting for transfers between devices: 34.1 us -> 14.4 us
  starting transfers between devices: 28.3 us -> 12 us
  local copies, waits for them, and re-layouts: 6.77 us -> 3.9 us
    all_to_all x0 -> x1, blocking collectives: none -> 40.2 us  [exchange(): return lax.all_to_all(blocks, axis, split_axis=0, concat_axis=0, tiled=True)]
    all_to_all x3 -> x2, waiting for transfers between devices: 33.9 us -> 9.9 us  [exchange(): return lax.all_to_all(blocks, axis, split_axis=0, concat_axis=0, tiled=True)]
    all_to_all x3 -> x2, starting transfers between devices: 27.1 us -> 10.7 us  [exchange(): return lax.all_to_all(blocks, axis, split_axis=0, concat_axis=0, tiled=True)]
    ppermute x1, waiting for transfers between devices: 0.19 us -> 4.5 us  [shifted(): return lax.ppermute(shard, axis, pairs)]
    unnamed x10 -> x6, local copies, waits for them, and re-layouts: 4.51 us -> 2.51 us
    pallas_call x1, Pallas kernels: 2.66 us -> 3.96 us  [pool(): pl.pallas_call(pool_kernel, out_shape=jax.ShapeDtypeStruct((copies, patch...]
    pallas_call x2 -> x1, Pallas kernels: 2.5 us -> 2.93 us  [prepare(): pl.pallas_call(prepare_kernel, out_shape=(jax.ShapeDtypeStruct((copies, R...]
  transfers between devices with their start and end apart: 4 -> 3, of which waited for: 3 -> 2; matrix products, arithmetic and copies ran while one was open for 0% -> 0% of each run, Pallas kernels for 3% -> 1%
where the time goes in v4:
time: 126 us
  blocking collectives  83.5 us (66%)
  waiting for transfers between devices  14.4 us (11%)
  starting transfers between devices  12 us (10%)
  Pallas kernels  10.5 us (8%)
  local copies, waits for them, and re-layouts  3.9 us (3%)
    all_to_all x1, blocking collectives, exchange(): return lax.all_to_all(blocks, axis, split_axis=0, concat_axis=0, tiled=True)  40.2 us
    all_gather x1, blocking collectives, layer(): merged_all = lax.all_gather(merged, 'rep', axis=0, tiled=True)  22.3 us
    all_to_all x1, blocking collectives, layer(): lax.all_to_all(attended, 'seq', split_axis=0, concat_axis=1, tiled=True)  20.9 us
    all_to_all x2, starting transfers between devices, exchange(): return lax.all_to_all(blocks, axis, split_axis=0, concat_axis=0, tiled=True)  10.7 us
    all_to_all x2, waiting for transfers between devices, exchange(): return lax.all_to_all(blocks, axis, split_axis=0, concat_axis=0, tiled=True)  9.9 us
    ppermute x1, waiting for transfers between devices, shifted(): return lax.ppermute(shard, axis, pairs)  4.5 us
    pallas_call x1, Pallas kernels, pool(): pl.pallas_call(pool_kernel, out_shape=jax.ShapeDtypeStruct((copies, patch...  3.96 us
    pallas_call x1, Pallas kernels, prepare(): pl.pallas_call(prepare_kernel, out_shape=(jax.ShapeDtypeStruct((copies, R...  2.93 us
  transfers between devices with their start and end apart: 3, of which 2 were waited for; matrix products, arithmetic and copies ran while one was open for 0% of the time, Pallas kernels for 1%

profile of v4, /device:TPU:1, one launch (start us, length us, event | category | flops | bytes accessed | tf_op | source)
XLA Modules:
  0.0 125.5 jit_solution(7896506392756136447)
XLA Ops:
  0.0 0.0 copy-start.1
  0.7 2.9 %prepare.1 = (bf16[32,32,128]{2,1,0:T(8,128)(2,1)}, bf16[64,512]{1,0:T(8,128)(2,1)}, bf16[192,512]{1,0:T(8,128)(2,1)}, s32[32,128]{1,0:T(8,128)}, s32[32,128]{1,...) custom-call(s32[1]{0:T(128)} %bitcast.index_ref, s32[1]{0:T(128)} %bitcast.1.base_ref, s32[32]{0:T(128)} %starts_ref.1, ...), custom_call_target="tpu_custom_call" | custom-call | tf_op jit(solution)/shard_map/prepare/pallas_call | solution.py:81
  3.6 1.3 %collective-permute-start = (bf16[64,512]{1,0:T(8,128)(2,1)}, bf16[64,512]{1,0:T(8,128)(2,1)S(1)}, u32[]{:S(2)}, u32[]{:S(2)}) collective-permute-start(bf16[64,512]{1,0:T(8,128)(2,1)} %get-tuple-element.15), channel_id=1, source_target_pairs={{16,0},{32,16},{48,32},{64,48},{80,64},{96,80},{112,96},{128,112},... | collective-permute-start | bytes 196616 | tf_op jit(solution)/shard_map/ppermute | solution.py:25
  4.9 4.5 %collective-permute-done.halo_ref = bf16[64,512]{1,0:T(8,128)(2,1)S(1)} collective-permute-done((bf16[64,512]{1,0:T(8,128)(2,1)}, bf16[64,512]{1,0:T(8,128)(2,1)S(1)}, u32[]{:S(2)}, u32[]{:S(2)}) %collective-permute-start) | collective-permute-done | bytes 65568 | tf_op jit(solution)/shard_map/ppermute | solution.py:25
  9.4 0.0 copy-start.2
  9.4 0.6 copy-done.2
  10.0 4.0 %pool.1 = bf16[32,32,512]{2,1,0:T(8,128)(2,1)} custom-call(s32[32,128]{1,0:T(8,128)} %get-tuple-element.12.first_ref, s32[32,128]{1,0:T(8,128)} %get-tuple-element.13.end_ref, bf16[192,512]{1,0:T(8,128)(2,1)} %get-tuple-element.14.states_ref, bf16[64,512]{1,0:T(8,128)(2,1)} %copy-done.2, bf16[192,512]{1,0:T(8,128)(2,1)} %get-tuple-element.16.keys_ref, ...), custom_call_target="tpu_custom_call" | custom-call | tf_op jit(solution)/shard_map/pool/pallas_call | solution.py:143
  14.0 40.2 %all_to_all.34 = bf16[32,32,512]{2,1,0:T(8,128)(2,1)S(1)} all-to-all(bf16[32,32,512]{2,1,0:T(8,128)(2,1)} %pool.1), channel_id=1, replica_groups=mesh['seq'=32,'rep'=16] {'seq'}, dimensions={0} | all-to-all | bytes 2097152 | tf_op jit(solution)/shard_map/all_to_all | solution.py:259
  54.2 6.8 %all-to-all-start.2 = ((bf16[32,32,128]{2,1,0:T(8,128)(2,1)}), bf16[32,32,128]{2,1,0:T(8,128)(2,1)S(1)}, u32[]{:S(2)}, u32[]{:S(2)}) async-start(bf16[32,32,128]{2,1,0:T(8,128)(2,1)} %get-tuple-element.18), calls=%async_computation.2 | async-start | bytes 524288 | tf_op jit(solution)/shard_map/all_to_all | solution.py:259
  61.1 0.0 copy-done.1
  61.1 0.5 fusion
  61.6 9.9 %all-to-all-done.2.blocks_ref = bf16[32,32,128]{2,1,0:T(8,128)(2,1)S(1)} async-done(((bf16[32,32,128]{2,1,0:T(8,128)(2,1)}), bf16[32,32,128]{2,1,0:T(8,128)(2,1)S(1)}, u32[]{:S(2)}, u32[]{:S(2)}) %all-to-all-start.2) | async-done | bytes 262176 | tf_op jit(solution)/shard_map/all_to_all | solution.py:259
  71.5 0.7 broadcast_in_dim.8
  72.1 3.9 %all-to-all-start.1 = ((f32[32,8,128]{2,1,0:T(8,128)}), f32[32,8,128]{2,1,0:T(8,128)S(1)}, u32[]{:S(2)}, u32[]{:S(2)}) async-start(f32[32,8,128]{2,1,0:T(8,128)} %broadcast_in_dim.8), calls=%async_computation.1 | async-start | bytes 262144 | tf_op jit(solution)/shard_map/all_to_all | solution.py:259
  76.0 0.0 copy-start
  76.0 1.9 %copy-done = bf16[4096,3,128]{2,0,1:T(8,128)(2,1)S(1)} copy-done((bf16[4096,3,128]{2,0,1:T(8,128)(2,1)S(1)}, bf16[4096,3,128]{2,0,1:T(8,128)(2,1)}, u32[]{:S(2)}) %copy-start) | copy-done | bytes 3145752
  77.9 1.2 merge.1
  79.1 22.3 %all_gather.3.merged_ref = bf16[512,384]{1,0:T(8,128)(2,1)S(1)} all-gather(bf16[32,384]{1,0:T(8,128)(2,1)S(1)} %merge.1), channel_id=1, replica_groups=mesh['seq'=32,'rep'=16] {'rep'}, dimensions={0}, use_global_device_ids=true | all-gather | bytes 417792 | tf_op jit(solution)/shard_map/all_gather | solution.py:277
  101.5 0.0 all-to-all-done.1.square_ref
  101.5 2.4 %attend.1 = bf16[1024,128]{1,0:T(8,128)(2,1)S(1)} custom-call(f32[32,8,128]{2,1,0:T(8,128)S(1)} %all-to-all-done.1.square_ref, bf16[1024,512]{1,0:T(8,128)(2,1)S(1)} %bitcast.16, bf16[512,384]{1,0:T(8,128)(2,1)S(1)} %all_gather.3.merged_ref), custom_call_target="tpu_custom_call" | custom-call | tf_op jit(solution)/shard_map/attend/pallas_call | solution.py:247
  103.9 20.9 %all_to_all.35 = bf16[32,32,128]{2,1,0:T(8,128)(2,1)S(1)} all-to-all(bf16[32,32,128]{2,1,0:T(8,128)(2,1)S(1)} %bitcast.18), channel_id=1, replica_groups=mesh['seq'=32,'rep'=16] {'seq'}, dimensions={0} | all-to-all | bytes 524288 | tf_op jit(solution)/shard_map/all_to_all | solution.py:284
  124.8 0.7 copy_bitcast_fusion
Async XLA Ops:
  0.0 61.1 %copy-start.1 = (bf16[512,128]{1,0:T(8,128)(2,1)S(1)}, bf16[512,128]{1,0:T(8,128)(2,1)}, u32[]{:S(2)}) copy-start(bf16[512,128]{1,0:T(8,128)(2,1)} %out_weight_ref.1) | copy-start | bytes 393220
  3.6 5.8 %collective-permute-start = (bf16[64,512]{1,0:T(8,128)(2,1)}, bf16[64,512]{1,0:T(8,128)(2,1)S(1)}, u32[]{:S(2)}, u32[]{:S(2)}) collective-permute-start(bf16[64,512]{1,0:T(8,128)(2,1)} %get-tuple-element.15), channel_id=1, source_target_pairs={{16,0},{32,16},{48,32},{64,48},{80,64},{96,80},{112,96},{128,112},... | collective-permute-start | bytes 196616 | tf_op jit(solution)/shard_map/ppermute | solution.py:25
  9.4 0.6 copy-start.2
  54.2 17.2 %all-to-all-start.2 = ((bf16[32,32,128]{2,1,0:T(8,128)(2,1)}), bf16[32,32,128]{2,1,0:T(8,128)(2,1)S(1)}, u32[]{:S(2)}, u32[]{:S(2)}) async-start(bf16[32,32,128]{2,1,0:T(8,128)(2,1)} %get-tuple-element.18), calls=%async_computation.2 | async-start | bytes 524288 | tf_op jit(solution)/shard_map/all_to_all | solution.py:259
  72.1 29.3 %all-to-all-start.1 = ((f32[32,8,128]{2,1,0:T(8,128)}), f32[32,8,128]{2,1,0:T(8,128)S(1)}, u32[]{:S(2)}, u32[]{:S(2)}) async-start(f32[32,8,128]{2,1,0:T(8,128)} %broadcast_in_dim.8), calls=%async_computation.1 | async-start | bytes 262144 | tf_op jit(solution)/shard_map/all_to_all | solution.py:259
  76.0 1.9 %copy-start = (bf16[4096,3,128]{2,0,1:T(8,128)(2,1)S(1)}, bf16[4096,3,128]{2,0,1:T(8,128)(2,1)}, u32[]{:S(2)}) copy-start(bf16[4096,3,128]{2,0,1:T(8,128)(2,1)} %param.13) | copy-start | bytes 9437188

commit v5 on v4

--- a/solution.py
+++ b/solution.py
@@ -33,21 +33,48 @@
     return [pl.BlockSpec(memory_space=pltpu.SMEM)] * count
 
 
-def prepare_kernel(
-    index_ref, base_ref, starts_ref, straddle_ref, out_weight_ref, gain_ref, states_ref, weight_ref,
-    blocks_ref, halo_ref, keys_ref, first_ref, end_ref, own_ref, own_weight_ref,
-    rows_ref, columns_ref, sems,
-):
-    start = pl.multiple_of(index_ref[0] * ROWS, ROWS)
-    copies = [
-        pltpu.make_async_copy(out_weight_ref.at[pl.ds(start, ROWS), :], rows_ref, sems.at[0]),
-        pltpu.make_async_copy(gain_ref, columns_ref, sems.at[1]),
-        pltpu.make_async_copy(states_ref, own_ref, sems.at[2]),
-        pltpu.make_async_copy(weight_ref, own_weight_ref, sems.at[3]),
-    ]
-    for copy in copies:
-        copy.start()
+def rows_kernel(index_ref, weight_ref, gain_ref, states_ref, out_ref, edge_ref):
+    block = (weight_ref[...].astype(jnp.float32) * gain_ref[...].astype(jnp.float32)).astype(
+        jnp.bfloat16
+    )
+    for target in range(out_ref.shape[0]):
+        out_ref[target] = block
+    edge_ref[...] = states_ref[...]
+
+
+def weight_rows(out_weight, norm_gain, states, index, copies):
+    columns, width = out_weight.shape[1], states.shape[1]
+    return pl.pallas_call(
+        rows_kernel,
+        out_shape=(
+            jax.ShapeDtypeStruct((copies, ROWS, columns), jnp.bfloat16),
+            jax.ShapeDtypeStruct((HALO, width), jnp.bfloat16),
+        ),
+        grid_spec=pltpu.PrefetchScalarGridSpec(
+            num_scalar_prefetch=1,
+            grid=(1,),
+            in_specs=[
+                pl.BlockSpec((ROWS, columns), lambda step, index: (index[0], 0)),
+                pl.BlockSpec((1, columns), lambda step, index: (0, 0)),
+                pl.BlockSpec((HALO, width), lambda step, index: (0, 0)),
+            ],
+            out_specs=[
+                pl.BlockSpec((copies, ROWS, columns), lambda step, index: (0, 0, 0)),
+                pl.BlockSpec((HALO, width), lambda step, index: (0, 0)),
+            ],
+        ),
+        name="rows",
+    )(index.reshape(1), out_weight, norm_gain.reshape(1, -1), states)
+
+
+def keys_kernel(base_ref, starts_ref, straddle_ref, states_ref, weight_ref, keys_ref, first_ref, end_ref, states_out, weight_out):
     patches = first_ref.shape[0]
+    shard_bytes = states_ref.shape[0]
+    keys_ref[...] = jnp.dot(
+        states_ref[...], weight_ref[...], preferred_element_type=jnp.float32
+    ).astype(jnp.bfloat16)
+    states_out[...] = states_ref[...]
+    weight_out[...] = weight_ref[...]
     row = lax.broadcasted_iota(jnp.int32, first_ref.shape, 0)
     first = jnp.zeros(first_ref.shape, jnp.int32)
     end = jnp.zeros(first_ref.shape, jnp.int32)
@@ -58,49 +85,26 @@
         if patch > 0:
             end = jnp.where(row == patch - 1, begin, end)
     first_ref[...] = first
-    end_ref[...] = jnp.where(row == patches - 1, own_ref.shape[0] + straddle_ref[0], end)
-    copies[0].wait()
-    copies[1].wait()
-    block = (
-        rows_ref[...].astype(jnp.float32) * columns_ref[...].astype(jnp.float32)
-    ).astype(jnp.bfloat16)
-    for target in range(blocks_ref.shape[0]):
-        blocks_ref[target] = block
-    copies[2].wait()
-    halo_ref[...] = own_ref[:HALO, :]
-    copies[3].wait()
-    keys_ref[...] = jnp.dot(
-        own_ref[...], own_weight_ref[...], preferred_element_type=jnp.float32
-    ).astype(jnp.bfloat16)
-
-
-def prepare(index, base, starts, straddle, out_weight, norm_gain, states, key_weight, copies):
-    patches, width = starts.shape[0], states.shape[1]
-    columns = out_weight.shape[1]
+    end_ref[...] = jnp.where(row == patches - 1, shard_bytes + straddle_ref[0], end)
+
+
+def own_keys(base, starts, straddle, states, key_weight):
+    patches = starts.shape[0]
     bounds = jax.ShapeDtypeStruct((patches, 128), jnp.int32)
     return pl.pallas_call(
-        prepare_kernel,
+        keys_kernel,
         out_shape=(
-            jax.ShapeDtypeStruct((copies, ROWS, columns), jnp.bfloat16),
-            jax.ShapeDtypeStruct((HALO, width), jnp.bfloat16),
             jax.ShapeDtypeStruct(states.shape, jnp.bfloat16),
             bounds,
             bounds,
             jax.ShapeDtypeStruct(states.shape, jnp.bfloat16),
             jax.ShapeDtypeStruct(key_weight.shape, jnp.bfloat16),
         ),
-        in_specs=scalars(4) + [pl.BlockSpec(memory_space=pltpu.HBM)] * 4,
-        out_specs=tuple(whole(7)),
-        scratch_shapes=[
-            pltpu.VMEM((ROWS, columns), jnp.bfloat16),
-            pltpu.VMEM((1, columns), jnp.bfloat16),
-            pltpu.SemaphoreType.DMA((4,)),
-        ],
-        name="prepare",
-    )(
-        index.reshape(1), base.reshape(1), starts, straddle,
-        out_weight, norm_gain.reshape(1, -1), states, key_weight,
-    )
+        in_specs=scalars(3) + whole(2),
+        out_specs=tuple(whole(5)),
+        compiler_params=pltpu.CompilerParams(vmem_limit_bytes=8 << 20),
+        name="own_keys",
+    )(base.reshape(1), starts, straddle, states, key_weight)
 
 
 def pool_kernel(first_ref, end_ref, states_ref, halo_ref, keys_ref, weight_ref, out_ref):
@@ -145,6 +149,7 @@
         out_shape=jax.ShapeDtypeStruct((copies, patches, width), jnp.bfloat16),
         in_specs=whole(6),
         out_specs=pl.BlockSpec(memory_space=pltpu.VMEM),
+        compiler_params=pltpu.CompilerParams(vmem_limit_bytes=16 << 20),
         name="pool",
     )(first, end, states, halo, keys, key_weight)
 
@@ -265,12 +270,10 @@
     model_width = attn_weight.shape[0]
     pooled_width = out_weight.shape[0]
 
-    row_blocks, edge, keys, first, end, own, weight = prepare(
-        lax.axis_index("rep"), base, starts, straddle,
-        out_weight, norm_gain, states, key_weight, seq,
-    )
+    row_blocks, edge = weight_rows(out_weight, norm_gain, states, lax.axis_index("rep"), seq)
     weight_blocks = exchange(row_blocks, "seq")
     halo_rows = shifted(edge, "seq", -1)
+    keys, first, end, own, weight = own_keys(base, starts, straddle, states, key_weight)
     pooled_blocks = pool(first, end, own, halo_rows, keys, weight, seq)
     pooled_all = exchange(pooled_blocks, "seq").reshape(-1, pooled_width)
     merged = merge_weights(weight_blocks, attn_weight)

time: 126 us -> 121 us (0.960)
  waiting for transfers between devices: 14.4 us -> 10.3 us
  Pallas kernels: 10.5 us -> 7.76 us
  local copies, waits for them, and re-layouts: 3.9 us -> 5.89 us
    ppermute x1, waiting for transfers between devices: 4.5 us -> 0.41 us  [shifted(): return lax.ppermute(shard, axis, pairs)]
    pallas_call x1, Pallas kernels: 3.96 us -> 1.67 us  [pool(): pl.pallas_call(pool_kernel, out_shape=jax.ShapeDtypeStruct((copies, patch...]
    unnamed x6 -> x10, local copies, waits for them, and re-layouts: 2.51 us -> 4.51 us
    pallas_call x1 -> x2, Pallas kernels: 2.93 us -> 2.44 us  [the longest x1 1.64 us: weight_rows(): pl.pallas_call(rows_kernel, out_shape=(jax.ShapeDtypeStruct((copies, ROWS...]
  transfers between devices with their start and end apart: 3 -> 3, of which waited for: 2 -> 2; matrix products, arithmetic and copies ran while one was open for 0% -> 0% of each run, Pallas kernels for 1% -> 2%
where the time goes in v5:
time: 121 us; the launch traced here: 120 us
  blocking collectives  83.3 us (69%)
  starting transfers between devices  12 us (10%)
  waiting for transfers between devices  10.3 us (9%)
  Pallas kernels  7.76 us (6%)
  local copies, waits for them, and re-layouts  5.89 us (5%)
    all_to_all x1, blocking collectives, exchange(): return lax.all_to_all(blocks, axis, split_axis=0, concat_axis=0, tiled=True)  40 us
    all_gather x1, blocking collectives, layer(): merged_all = lax.all_gather(merged, 'rep', axis=0, tiled=True)  22.3 us
    all_to_all x1, blocking collectives, layer(): lax.all_to_all(attended, 'seq', split_axis=0, concat_axis=1, tiled=True)  20.9 us
    all_to_all x2, starting transfers between devices, exchange(): return lax.all_to_all(blocks, axis, split_axis=0, concat_axis=0, tiled=True)  10.7 us
    all_to_all x2, waiting for transfers between devices, exchange(): return lax.all_to_all(blocks, axis, split_axis=0, concat_axis=0, tiled=True)  9.9 us
    unnamed x10, local copies, waits for them, and re-layouts  4.51 us
  transfers between devices with their start and end apart: 3, of which 2 were waited for; matrix products, arithmetic and copies ran while one was open for 0% of the time, Pallas kernels for 2%

profile of v5, /device:TPU:1, one launch (start us, length us, event | category | flops | bytes accessed | tf_op | source)
XLA Modules:
  0.0 120.4 jit_solution(17126465895772929585)
XLA Ops:
  0.0 0.0 copy-start.4
  0.0 1.6 %rows.1 = (bf16[32,32,128]{2,1,0:T(8,128)(2,1)}, bf16[64,512]{1,0:T(8,128)(2,1)}) custom-call(s32[1]{0:T(128)} %bitcast.1.index_ref, bf16[512,128]{1,0:T(8,128)(2,1)} %weight_ref.3, bf16[1,128]{1,0:T(2,128)(2,1)} %bitcast.20, bf16[192,512]{1,0:T(8,128)(2,1)} %states_ref.3), custom_call_target="tpu_custom_call" | custom-call | tf_op jit(solution)/shard_map/rows/pallas_call | solution.py:47
  1.6 1.3 %collective-permute-start = (bf16[64,512]{1,0:T(8,128)(2,1)}, bf16[64,512]{1,0:T(8,128)(2,1)S(1)}, u32[]{:S(2)}, u32[]{:S(2)}) collective-permute-start(bf16[64,512]{1,0:T(8,128)(2,1)} %get-tuple-element.15), channel_id=1, source_target_pairs={{16,0},{32,16},{48,32},{64,48},{80,64},{96,80},{112,96},{128,112},... | collective-permute-start | bytes 196616 | tf_op jit(solution)/shard_map/ppermute | solution.py:25
  3.6 0.0 copy-start.1
  3.6 0.9 copy-done.1
  4.5 0.0 copy-start.2
  4.5 1.0 copy-done.2
  5.6 0.0 copy-start.3
  5.6 0.7 copy-done.3
  6.2 0.8 own_keys.1
  7.0 0.4 collective-permute-done.halo_ref
  7.4 1.7 %pool.1 = bf16[32,32,512]{2,1,0:T(8,128)(2,1)S(1)} custom-call(s32[32,128]{1,0:T(8,128)S(1)} %get-tuple-element.12.first_ref, s32[32,128]{1,0:T(8,128)S(1)} %get-tuple-element.13.end_ref, bf16[192,512]{1,0:T(8,128)(2,1)S(1)} %get-tuple-element.14.states_ref, bf16[64,512]{1,0:T(8,128)(2,1)S(1)} %collective-permute-done.halo_ref, ...), custom_call_target="tpu_custom_call" | custom-call | tf_op jit(solution)/shard_map/pool/pallas_call | solution.py:147
  9.1 40.0 %all_to_all.34 = bf16[32,32,512]{2,1,0:T(8,128)(2,1)S(1)} all-to-all(bf16[32,32,512]{2,1,0:T(8,128)(2,1)S(1)} %pool.1), channel_id=1, replica_groups=mesh['seq'=32,'rep'=16] {'seq'}, dimensions={0} | all-to-all | bytes 2097152 | tf_op jit(solution)/shard_map/all_to_all | solution.py:264
  49.1 6.8 %all-to-all-start.2 = ((bf16[32,32,128]{2,1,0:T(8,128)(2,1)}), bf16[32,32,128]{2,1,0:T(8,128)(2,1)S(1)}, u32[]{:S(2)}, u32[]{:S(2)}) async-start(bf16[32,32,128]{2,1,0:T(8,128)(2,1)} %get-tuple-element.18), calls=%async_computation.2 | async-start | bytes 524288 | tf_op jit(solution)/shard_map/all_to_all | solution.py:264
  56.0 0.0 copy-done.4
  56.0 0.5 fusion
  56.5 9.9 %all-to-all-done.2.blocks_ref = bf16[32,32,128]{2,1,0:T(8,128)(2,1)S(1)} async-done(((bf16[32,32,128]{2,1,0:T(8,128)(2,1)}), bf16[32,32,128]{2,1,0:T(8,128)(2,1)S(1)}, u32[]{:S(2)}, u32[]{:S(2)}) %all-to-all-start.2) | async-done | bytes 262176 | tf_op jit(solution)/shard_map/all_to_all | solution.py:264
  66.4 0.7 broadcast_in_dim.8
  67.0 3.9 %all-to-all-start.1 = ((f32[32,8,128]{2,1,0:T(8,128)}), f32[32,8,128]{2,1,0:T(8,128)S(1)}, u32[]{:S(2)}, u32[]{:S(2)}) async-start(f32[32,8,128]{2,1,0:T(8,128)} %broadcast_in_dim.8), calls=%async_computation.1 | async-start | bytes 262144 | tf_op jit(solution)/shard_map/all_to_all | solution.py:264
  70.9 0.0 copy-start
  70.9 1.9 %copy-done = bf16[4096,3,128]{2,0,1:T(8,128)(2,1)S(1)} copy-done((bf16[4096,3,128]{2,0,1:T(8,128)(2,1)S(1)}, bf16[4096,3,128]{2,0,1:T(8,128)(2,1)}, u32[]{:S(2)}) %copy-start) | copy-done | bytes 3145752
  72.8 1.2 %merge.1 = bf16[32,384]{1,0:T(8,128)(2,1)S(1)} custom-call(bf16[32,32,128]{2,1,0:T(8,128)(2,1)S(1)} %all-to-all-done.2.blocks_ref, bf16[3,4096,128]{2,1,0:T(8,128)(2,1)S(1)} %bitcast.17), custom_call_target="tpu_custom_call" | custom-call | tf_op jit(solution)/shard_map/merge/pallas_call | solution.py:181
  74.0 22.3 %all_gather.3.merged_ref = bf16[512,384]{1,0:T(8,128)(2,1)S(1)} all-gather(bf16[32,384]{1,0:T(8,128)(2,1)S(1)} %merge.1), channel_id=1, replica_groups=mesh['seq'=32,'rep'=16] {'rep'}, dimensions={0}, use_global_device_ids=true | all-gather | bytes 417792 | tf_op jit(solution)/shard_map/all_gather | solution.py:280
  96.4 0.0 all-to-all-done.1.square_ref
  96.4 2.4 %attend.1 = bf16[1024,128]{1,0:T(8,128)(2,1)S(1)} custom-call(f32[32,8,128]{2,1,0:T(8,128)S(1)} %all-to-all-done.1.square_ref, bf16[1024,512]{1,0:T(8,128)(2,1)S(1)} %bitcast.16, bf16[512,384]{1,0:T(8,128)(2,1)S(1)} %all_gather.3.merged_ref), custom_call_target="tpu_custom_call" | custom-call | tf_op jit(solution)/shard_map/attend/pallas_call | solution.py:252
  98.8 20.9 %all_to_all.35 = bf16[32,32,128]{2,1,0:T(8,128)(2,1)S(1)} all-to-all(bf16[32,32,128]{2,1,0:T(8,128)(2,1)S(1)} %bitcast.18), channel_id=1, replica_groups=mesh['seq'=32,'rep'=16] {'seq'}, dimensions={0} | all-to-all | bytes 524288 | tf_op jit(solution)/shard_map/all_to_all | solution.py:287
  119.7 0.7 copy_bitcast_fusion
Async XLA Ops:
  0.0 56.0 %copy-start.4 = (bf16[512,128]{1,0:T(8,128)(2,1)S(1)}, bf16[512,128]{1,0:T(8,128)(2,1)}, u32[]{:S(2)}) copy-start(bf16[512,128]{1,0:T(8,128)(2,1)} %weight_ref.3) | copy-start | bytes 393220
  1.6 5.8 %collective-permute-start = (bf16[64,512]{1,0:T(8,128)(2,1)}, bf16[64,512]{1,0:T(8,128)(2,1)S(1)}, u32[]{:S(2)}, u32[]{:S(2)}) collective-permute-start(bf16[64,512]{1,0:T(8,128)(2,1)} %get-tuple-element.15), channel_id=1, source_target_pairs={{16,0},{32,16},{48,32},{64,48},{80,64},{96,80},{112,96},{128,112},... | collective-permute-start | bytes 196616 | tf_op jit(solution)/shard_map/ppermute | solution.py:25
  3.6 0.9 copy-start.1
  4.5 1.0 copy-start.2
  5.6 0.7 copy-start.3
  49.1 17.2 %all-to-all-start.2 = ((bf16[32,32,128]{2,1,0:T(8,128)(2,1)}), bf16[32,32,128]{2,1,0:T(8,128)(2,1)S(1)}, u32[]{:S(2)}, u32[]{:S(2)}) async-start(bf16[32,32,128]{2,1,0:T(8,128)(2,1)} %get-tuple-element.18), calls=%async_computation.2 | async-start | bytes 524288 | tf_op jit(solution)/shard_map/all_to_all | solution.py:264
  67.0 29.3 %all-to-all-start.1 = ((f32[32,8,128]{2,1,0:T(8,128)}), f32[32,8,128]{2,1,0:T(8,128)S(1)}, u32[]{:S(2)}, u32[]{:S(2)}) async-start(f32[32,8,128]{2,1,0:T(8,128)} %broadcast_in_dim.8), calls=%async_computation.1 | async-start | bytes 262144 | tf_op jit(solution)/shard_map/all_to_all | solution.py:264
  70.9 1.9 %copy-start = (bf16[4096,3,128]{2,0,1:T(8,128)(2,1)S(1)}, bf16[4096,3,128]{2,0,1:T(8,128)(2,1)}, u32[]{:S(2)}) copy-start(bf16[4096,3,128]{2,0,1:T(8,128)(2,1)} %param.13) | copy-start | bytes 9437188

commit v6 on v5

--- a/solution.py
+++ b/solution.py
@@ -12,6 +12,7 @@
 LHD = 128
 HALO = 64
 ROWS = 32
+ALONG_X = 4
 TILE = 256
 WIDE = 512
 
@@ -164,7 +165,7 @@
     rows = jnp.concatenate([blocks_ref[shard] for shard in range(blocks_ref.shape[0])], axis=1)
     for part in range(weight_ref.shape[0]):
         total_ref[:, part * HD : (part + 1) * HD] += jnp.dot(
-            rows, weight_ref[part], preferred_element_type=jnp.float32
+            rows, weight_ref[part].reshape(rows.shape[1], -1), preferred_element_type=jnp.float32
         )
 
     @pl.when(step == pl.num_programs(0) - 1)
@@ -173,24 +174,21 @@
 
 
 def merge_weights(blocks, attn_weight):
-    shards_total, block_rows, columns = blocks.shape
-    steps = 4
-    group = shards_total // steps
     planes = jnp.swapaxes(attn_weight, 0, 1)
+    steps, group, _, columns = blocks.shape
     parts, _, width = planes.shape
     return pl.pallas_call(
         merge_kernel,
         out_shape=jax.ShapeDtypeStruct((ROWS, parts * width), jnp.bfloat16),
         grid=(steps,),
         in_specs=[
-            pl.BlockSpec((group, block_rows, columns), lambda s: (s, 0, 0)),
-            pl.BlockSpec((parts, group * columns, width), lambda s: (0, s, 0)),
+            pl.BlockSpec((None, group, ROWS, columns), lambda s: (s, 0, 0, 0)),
+            pl.BlockSpec((parts, group, None, columns, width), lambda s: (0, 0, s, 0, 0)),
         ],
         out_specs=pl.BlockSpec((ROWS, parts * width), lambda s: (0, 0)),
         scratch_shapes=[pltpu.VMEM((ROWS, parts * width), jnp.float32)],
-        compiler_params=pltpu.CompilerParams(vmem_limit_bytes=16 << 20),
         name="merge",
-    )(blocks, planes)
+    )(blocks, planes.reshape(parts, group, steps, columns, width))
 
 
 def attend_kernel(model_width, square_ref, pooled_ref, merged_ref, out_ref, view_ref):
@@ -269,13 +267,26 @@
     base = lax.axis_index("seq") * states.shape[0]
     model_width = attn_weight.shape[0]
     pooled_width = out_weight.shape[0]
-
-    row_blocks, edge = weight_rows(out_weight, norm_gain, states, lax.axis_index("rep"), seq)
-    weight_blocks = exchange(row_blocks, "seq")
+    lines = [list(range(i, i + ALONG_X)) for i in range(0, seq, ALONG_X)]
+    columns = [list(range(i, seq, ALONG_X)) for i in range(ALONG_X)]
+
+    row_blocks, edge = weight_rows(
+        out_weight, norm_gain, states, lax.axis_index("rep"), seq // ALONG_X
+    )
+    column_blocks = lax.all_to_all(
+        row_blocks, "seq", split_axis=0, concat_axis=0, tiled=True, axis_index_groups=columns
+    )
     halo_rows = shifted(edge, "seq", -1)
     keys, first, end, own, weight = own_keys(base, starts, straddle, states, key_weight)
     pooled_blocks = pool(first, end, own, halo_rows, keys, weight, seq)
     pooled_all = exchange(pooled_blocks, "seq").reshape(-1, pooled_width)
+    weight_blocks = lax.all_gather(
+        column_blocks.reshape(-1, column_blocks.shape[2]),
+        "seq",
+        axis=0,
+        tiled=True,
+        axis_index_groups=lines,
+    ).reshape(ALONG_X, *column_blocks.shape)
     merged = merge_weights(weight_blocks, attn_weight)
     merged_all = lax.all_gather(merged, "rep", axis=0, tiled=True)
     part = lax.dot_general(

time: 121 us -> 130 us (1.074)
  blocking collectives: 83.3 us -> 96.7 us
  waiting for transfers between devices: 10.3 us -> 7.14 us
  Pallas kernels: 7.76 us -> 10.2 us
  starting transfers between devices: 12 us -> 10.1 us
  local copies, waits for them, and re-layouts: 5.89 us -> 4.01 us
    all_gather x0 -> x1, blocking collectives: none -> 10.7 us  [layer(): lax.all_gather(column_blocks.reshape(-1, column_blocks.shape[2]), 'seq',...]
    all_to_all x2 -> x1, waiting for transfers between devices: 9.9 us -> 0.01 us  [exchange(): return lax.all_to_all(blocks, axis, split_axis=0, concat_axis=0, tiled=True)]
    all_to_all x2 -> x1, starting transfers between devices: 10.7 us -> 3.86 us  [exchange(): return lax.all_to_all(blocks, axis, split_axis=0, concat_axis=0, tiled=True)]
    all_to_all x0 -> x1, waiting for transfers between devices: none -> 6.73 us  [layer(): lax.all_to_all(row_blocks, 'seq', split_axis=0, concat_axis=0, tiled=True...]
    all_to_all x0 -> x1, starting transfers between devices: none -> 4.98 us  [layer(): lax.all_to_all(row_blocks, 'seq', split_axis=0, concat_axis=0, tiled=True...]
    all_gather x1, blocking collectives: 22.3 us -> 26.1 us  [layer(): merged_all = lax.all_gather(merged, 'rep', axis=0, tiled=True)]
    pallas_call x1, Pallas kernels: 1.24 us -> 3.79 us  [merge_weights(): pl.pallas_call(merge_kernel, out_shape=jax.ShapeDtypeStruct((ROWS, parts...]
    unnamed x10 -> x8, local copies, waits for them, and re-layouts: 4.51 us -> 2.62 us
  transfers between devices with their start and end apart: 3 -> 3, of which waited for: 2 -> 2; matrix products, arithmetic and copies ran while one was open for 0% -> 0% of each run, Pallas kernels for 2% -> 4%
where the time goes in v6:
time: 130 us; the launch traced here: 129 us
  blocking collectives  96.7 us (74%)
  Pallas kernels  10.2 us (8%)
  starting transfers between devices  10.1 us (8%)
  waiting for transfers between devices  7.14 us (5%)
  local copies, waits for them, and re-layouts  4.01 us (3%)
    all_to_all x1, blocking collectives, exchange(): return lax.all_to_all(blocks, axis, split_axis=0, concat_axis=0, tiled=True)  40 us
    all_gather x1, blocking collectives, layer(): merged_all = lax.all_gather(merged, 'rep', axis=0, tiled=True)  26.1 us
    all_to_all x1, blocking collectives, layer(): lax.all_to_all(attended, 'seq', split_axis=0, concat_axis=1, tiled=True)  19.9 us
    all_gather x1, blocking collectives, layer(): lax.all_gather(column_blocks.reshape(-1, column_blocks.shape[2]), 'seq',...  10.7 us
    all_to_all x1, waiting for transfers between devices, layer(): lax.all_to_all(row_blocks, 'seq', split_axis=0, concat_axis=0, tiled=True...  6.73 us
    all_to_all x1, starting transfers between devices, layer(): lax.all_to_all(row_blocks, 'seq', split_axis=0, concat_axis=0, tiled=True...  4.98 us
    all_to_all x1, starting transfers between devices, exchange(): return lax.all_to_all(blocks, axis, split_axis=0, concat_axis=0, tiled=True)  3.86 us
    pallas_call x1, Pallas kernels, merge_weights(): pl.pallas_call(merge_kernel, out_shape=jax.ShapeDtypeStruct((ROWS, parts...  3.79 us
  transfers between devices with their start and end apart: 3, of which 2 were waited for; matrix products, arithmetic and copies ran while one was open for 0% of the time, Pallas kernels for 4%

profile of v6, /device:TPU:1, one launch (start us, length us, event | category | flops | bytes accessed | tf_op | source)
XLA Modules:
  0.0 129.4 jit_solution(6098074191060966652)
XLA Ops:
  0.0 0.0 copy-start.3
  0.0 1.6 %rows.1 = (bf16[8,32,128]{2,1,0:T(8,128)(2,1)}, bf16[64,512]{1,0:T(8,128)(2,1)}) custom-call(s32[1]{0:T(128)} %bitcast.1.index_ref, bf16[512,128]{1,0:T(8,128)(2,1)} %weight_ref.3, bf16[1,128]{1,0:T(2,128)(2,1)} %bitcast.26, bf16[192,512]{1,0:T(8,128)(2,1)} %states_ref.3), custom_call_target="tpu_custom_call" | custom-call | tf_op jit(solution)/shard_map/rows/pallas_call | solution.py:48
  1.6 1.3 collective-permute-start
  3.5 0.0 copy-start
  3.5 0.9 copy-done
  4.4 0.0 copy-start.1
  4.4 1.0 copy-done.1
  5.5 0.0 copy-start.2
  5.5 0.7 copy-done.2
  6.1 0.8 own_keys.1
  6.9 0.4 collective-permute-done.halo_ref
  7.4 1.7 %pool.1 = bf16[32,32,512]{2,1,0:T(8,128)(2,1)S(1)} custom-call(s32[32,128]{1,0:T(8,128)S(1)} %get-tuple-element.12.first_ref, s32[32,128]{1,0:T(8,128)S(1)} %get-tuple-element.13.end_ref, bf16[192,512]{1,0:T(8,128)(2,1)S(1)} %get-tuple-element.14.states_ref, bf16[64,512]{1,0:T(8,128)(2,1)S(1)} %collective-permute-done.halo_ref, ...), custom_call_target="tpu_custom_call" | custom-call | tf_op jit(solution)/shard_map/pool/pallas_call | solution.py:148
  9.0 40.0 %all_to_all.34 = bf16[32,32,512]{2,1,0:T(8,128)(2,1)S(1)} all-to-all(bf16[32,32,512]{2,1,0:T(8,128)(2,1)S(1)} %pool.1), channel_id=1, replica_groups=mesh['seq'=32,'rep'=16] {'seq'}, dimensions={0} | all-to-all | bytes 2097152 | tf_op jit(solution)/shard_map/all_to_all | solution.py:262
  49.1 5.0 %all-to-all-start.2 = ((bf16[8,32,128]{2,1,0:T(8,128)(2,1)}), bf16[8,32,128]{2,1,0:T(8,128)(2,1)S(1)}, u32[]{:S(2)}, u32[]{:S(2)}) async-start(bf16[8,32,128]{2,1,0:T(8,128)(2,1)} %get-tuple-element.18), calls=%async_computation.2 | async-start | bytes 131072 | tf_op jit(solution)/shard_map/all_to_all | solution.py:276
  54.0 0.0 copy-done.3
  54.0 0.5 fusion
  54.5 6.7 %all-to-all-done.2 = bf16[8,32,128]{2,1,0:T(8,128)(2,1)S(1)} async-done(((bf16[8,32,128]{2,1,0:T(8,128)(2,1)}), bf16[8,32,128]{2,1,0:T(8,128)(2,1)S(1)}, u32[]{:S(2)}, u32[]{:S(2)}) %all-to-all-start.2) | async-done | bytes 65568 | tf_op jit(solution)/shard_map/all_to_all | solution.py:276
  61.3 0.7 broadcast_in_dim.8
  61.9 3.9 %all-to-all-start.1 = ((f32[32,8,128]{2,1,0:T(8,128)}), f32[32,8,128]{2,1,0:T(8,128)S(1)}, u32[]{:S(2)}, u32[]{:S(2)}) async-start(f32[32,8,128]{2,1,0:T(8,128)} %broadcast_in_dim.8), calls=%async_computation.1 | async-start | bytes 262144 | tf_op jit(solution)/shard_map/all_to_all | solution.py:262
  65.8 10.7 %all_gather.6 = bf16[1024,128]{1,0:T(8,128)(2,1)} all-gather(bf16[256,128]{1,0:T(8,128)(2,1)S(1)} %bitcast.24), channel_id=1, replica_groups={{0,16,32,48},{64,80,96,112},{128,144,160,176},{192,208,224,240},{256,27..., dimensions={0}, use_global_device_ids=true | all-gather | bytes 327680 | tf_op jit(solution)/shard_map/all_gather | solution.py:283
  76.5 3.8 %merge.1 = bf16[32,384]{1,0:T(8,128)(2,1)} custom-call(bf16[4,8,32,128]{3,2,1,0:T(8,128)(2,1)} %bitcast.23, bf16[3,8,4,128,128]{4,3,2,1,0:T(8,128)(2,1)} %bitcast.22), custom_call_target="tpu_custom_call" | custom-call | tf_op jit(solution)/shard_map/merge/pallas_call | solution.py:180
  80.3 26.1 %all_gather.7.merged_ref = bf16[512,384]{1,0:T(8,128)(2,1)S(1)} all-gather(bf16[32,384]{1,0:T(8,128)(2,1)} %merge.1), channel_id=1, replica_groups=mesh['seq'=32,'rep'=16] {'rep'}, dimensions={0}, use_global_device_ids=true | all-gather | bytes 417792 | tf_op jit(solution)/shard_map/all_gather | solution.py:291
  106.4 0.0 all-to-all-done.1.square_ref
  106.4 2.4 %attend.1 = bf16[1024,128]{1,0:T(8,128)(2,1)S(1)} custom-call(f32[32,8,128]{2,1,0:T(8,128)S(1)} %all-to-all-done.1.square_ref, bf16[1024,512]{1,0:T(8,128)(2,1)S(1)} %bitcast.20, bf16[512,384]{1,0:T(8,128)(2,1)S(1)} %all_gather.7.merged_ref), custom_call_target="tpu_custom_call" | custom-call | tf_op jit(solution)/shard_map/attend/pallas_call | solution.py:250
  108.8 19.9 %all_to_all.35 = bf16[32,32,128]{2,1,0:T(8,128)(2,1)S(1)} all-to-all(bf16[32,32,128]{2,1,0:T(8,128)(2,1)S(1)} %bitcast.21), channel_id=1, replica_groups=mesh['seq'=32,'rep'=16] {'seq'}, dimensions={0} | all-to-all | bytes 524288 | tf_op jit(solution)/shard_map/all_to_all | solution.py:298
  128.7 0.7 copy_bitcast_fusion
Async XLA Ops:
  0.0 54.0 %copy-start.3 = (bf16[512,128]{1,0:T(8,128)(2,1)S(1)}, bf16[512,128]{1,0:T(8,128)(2,1)}, u32[]{:S(2)}) copy-start(bf16[512,128]{1,0:T(8,128)(2,1)} %weight_ref.3) | copy-start | bytes 393220
  1.6 5.8 %collective-permute-start = (bf16[64,512]{1,0:T(8,128)(2,1)}, bf16[64,512]{1,0:T(8,128)(2,1)S(1)}, u32[]{:S(2)}, u32[]{:S(2)}) collective-permute-start(bf16[64,512]{1,0:T(8,128)(2,1)} %get-tuple-element.15), channel_id=1, source_target_pairs={{16,0},{32,16},{48,32},{64,48},{80,64},{96,80},{112,96},{128,112},... | collective-permute-start | bytes 196616 | tf_op jit(solution)/shard_map/ppermute | solution.py:26
  3.5 0.9 copy-start
  4.4 1.0 copy-start.1
  5.5 0.7 copy-start.2
  49.1 12.2 %all-to-all-start.2 = ((bf16[8,32,128]{2,1,0:T(8,128)(2,1)}), bf16[8,32,128]{2,1,0:T(8,128)(2,1)S(1)}, u32[]{:S(2)}, u32[]{:S(2)}) async-start(bf16[8,32,128]{2,1,0:T(8,128)(2,1)} %get-tuple-element.18), calls=%async_computation.2 | async-start | bytes 131072 | tf_op jit(solution)/shard_map/all_to_all | solution.py:276
  61.9 44.4 %all-to-all-start.1 = ((f32[32,8,128]{2,1,0:T(8,128)}), f32[32,8,128]{2,1,0:T(8,128)S(1)}, u32[]{:S(2)}, u32[]{:S(2)}) async-start(f32[32,8,128]{2,1,0:T(8,128)} %broadcast_in_dim.8), calls=%async_computation.1 | async-start | bytes 262144 | tf_op jit(solution)/shard_map/all_to_all | solution.py:262

commit v7 on v5

--- a/solution.py
+++ b/solution.py
@@ -217,19 +217,27 @@
         jnp.int32, (TILE, TILE), 1
     )
     scale = jnp.float32(HD**-0.5)
-    for tile in range(patches // TILE):
+
+    def against(tile, first, last):
+        return lax.dot_general(
+            view_ref[tile * TILE : (tile + 1) * TILE, :HD],
+            view_ref[first * TILE : last * TILE, HD : 2 * HD],
+            (((1,), (1,)), ((), ())),
+            preferred_element_type=jnp.float32,
+        )
+
+    tiles = range(patches // TILE)
+    scores = [
+        (
+            jnp.where(causal, against(tile, tile, tile + 1), jnp.float32(-1e30)),
+            against(tile, 0, tile) if tile > 0 else None,
+        )
+        for tile in tiles
+    ]
+    for tile, (near, far) in zip(tiles, scores):
         rows = slice(tile * TILE, (tile + 1) * TILE)
-        query = view_ref[rows, :HD]
-
-        def against(keys):
-            return lax.dot_general(
-                query, keys, (((1,), (1,)), ((), ())), preferred_element_type=jnp.float32
-            )
-
-        near = jnp.where(causal, against(view_ref[rows, HD : 2 * HD]), jnp.float32(-1e30))
         peak = jnp.max(near, axis=1, keepdims=True)
         if tile > 0:
-            far = against(view_ref[: tile * TILE, HD : 2 * HD])
             peak = jnp.maximum(peak, jnp.max(far, axis=1, keepdims=True))
         near = jnp.exp((near - peak) * scale)
         total = jnp.sum(near, axis=1, keepdims=True)

time: 121 us -> 120 us (level)
  no operation moved by 1% of the time
where the time goes in v7:
time: 120 us
  blocking collectives  83.3 us (69%)
  starting transfers between devices  12 us (10%)
  waiting for transfers between devices  10.3 us (9%)
  Pallas kernels  7.11 us (6%)
  local copies, waits for them, and re-layouts  5.89 us (5%)
    all_to_all x1, blocking collectives, exchange(): return lax.all_to_all(blocks, axis, split_axis=0, concat_axis=0, tiled=True)  40 us
    all_gather x1, blocking collectives, layer(): merged_all = lax.all_gather(merged, 'rep', axis=0, tiled=True)  22.3 us
    all_to_all x1, blocking collectives, layer(): lax.all_to_all(attended, 'seq', split_axis=0, concat_axis=1, tiled=True)  20.9 us
    all_to_all x2, starting transfers between devices, exchange(): return lax.all_to_all(blocks, axis, split_axis=0, concat_axis=0, tiled=True)  10.7 us
    all_to_all x2, waiting for transfers between devices, exchange(): return lax.all_to_all(blocks, axis, split_axis=0, concat_axis=0, tiled=True)  9.9 us
    unnamed x10, local copies, waits for them, and re-layouts  4.51 us
  transfers between devices with their start and end apart: 3, of which 2 were waited for; matrix products, arithmetic and copies ran while one was open for 0% of the time, Pallas kernels for 2%

profile of v7, /device:TPU:1, one launch (start us, length us, event | category | flops | bytes accessed | tf_op | source)
XLA Modules:
  0.0 119.8 jit_solution(4525014993204816170)
XLA Ops:
  0.0 0.0 copy-start.4
  0.0 1.6 %rows.1 = (bf16[32,32,128]{2,1,0:T(8,128)(2,1)}, bf16[64,512]{1,0:T(8,128)(2,1)}) custom-call(s32[1]{0:T(128)} %bitcast.1.index_ref, bf16[512,128]{1,0:T(8,128)(2,1)} %weight_ref.3, bf16[1,128]{1,0:T(2,128)(2,1)} %bitcast.20, bf16[192,512]{1,0:T(8,128)(2,1)} %states_ref.3), custom_call_target="tpu_custom_call" | custom-call | tf_op jit(solution)/shard_map/rows/pallas_call | solution.py:47
  1.6 1.3 %collective-permute-start = (bf16[64,512]{1,0:T(8,128)(2,1)}, bf16[64,512]{1,0:T(8,128)(2,1)S(1)}, u32[]{:S(2)}, u32[]{:S(2)}) collective-permute-start(bf16[64,512]{1,0:T(8,128)(2,1)} %get-tuple-element.15), channel_id=1, source_target_pairs={{16,0},{32,16},{48,32},{64,48},{80,64},{96,80},{112,96},{128,112},... | collective-permute-start | bytes 196616 | tf_op jit(solution)/shard_map/ppermute | solution.py:25
  3.6 0.0 copy-start.1
  3.6 0.9 copy-done.1
  4.5 0.0 copy-start.2
  4.5 1.0 copy-done.2
  5.6 0.0 copy-start.3
  5.6 0.7 copy-done.3
  6.2 0.8 own_keys.1
  7.0 0.4 collective-permute-done.halo_ref
  7.4 1.7 %pool.1 = bf16[32,32,512]{2,1,0:T(8,128)(2,1)S(1)} custom-call(s32[32,128]{1,0:T(8,128)S(1)} %get-tuple-element.12.first_ref, s32[32,128]{1,0:T(8,128)S(1)} %get-tuple-element.13.end_ref, bf16[192,512]{1,0:T(8,128)(2,1)S(1)} %get-tuple-element.14.states_ref, bf16[64,512]{1,0:T(8,128)(2,1)S(1)} %collective-permute-done.halo_ref, ...), custom_call_target="tpu_custom_call" | custom-call | tf_op jit(solution)/shard_map/pool/pallas_call | solution.py:147
  9.1 40.0 %all_to_all.34 = bf16[32,32,512]{2,1,0:T(8,128)(2,1)S(1)} all-to-all(bf16[32,32,512]{2,1,0:T(8,128)(2,1)S(1)} %pool.1), channel_id=1, replica_groups=mesh['seq'=32,'rep'=16] {'seq'}, dimensions={0} | all-to-all | bytes 2097152 | tf_op jit(solution)/shard_map/all_to_all | solution.py:272
  49.1 6.8 %all-to-all-start.2 = ((bf16[32,32,128]{2,1,0:T(8,128)(2,1)}), bf16[32,32,128]{2,1,0:T(8,128)(2,1)S(1)}, u32[]{:S(2)}, u32[]{:S(2)}) async-start(bf16[32,32,128]{2,1,0:T(8,128)(2,1)} %get-tuple-element.18), calls=%async_computation.2 | async-start | bytes 524288 | tf_op jit(solution)/shard_map/all_to_all | solution.py:272
  56.0 0.0 copy-done.4
  56.0 0.5 fusion
  56.5 9.9 %all-to-all-done.2.blocks_ref = bf16[32,32,128]{2,1,0:T(8,128)(2,1)S(1)} async-done(((bf16[32,32,128]{2,1,0:T(8,128)(2,1)}), bf16[32,32,128]{2,1,0:T(8,128)(2,1)S(1)}, u32[]{:S(2)}, u32[]{:S(2)}) %all-to-all-start.2) | async-done | bytes 262176 | tf_op jit(solution)/shard_map/all_to_all | solution.py:272
  66.4 0.7 broadcast_in_dim.8
  67.0 3.9 %all-to-all-start.1 = ((f32[32,8,128]{2,1,0:T(8,128)}), f32[32,8,128]{2,1,0:T(8,128)S(1)}, u32[]{:S(2)}, u32[]{:S(2)}) async-start(f32[32,8,128]{2,1,0:T(8,128)} %broadcast_in_dim.8), calls=%async_computation.1 | async-start | bytes 262144 | tf_op jit(solution)/shard_map/all_to_all | solution.py:272
  70.9 0.0 copy-start
  70.9 1.9 %copy-done = bf16[4096,3,128]{2,0,1:T(8,128)(2,1)S(1)} copy-done((bf16[4096,3,128]{2,0,1:T(8,128)(2,1)S(1)}, bf16[4096,3,128]{2,0,1:T(8,128)(2,1)}, u32[]{:S(2)}) %copy-start) | copy-done | bytes 3145752
  72.8 1.2 %merge.1 = bf16[32,384]{1,0:T(8,128)(2,1)S(1)} custom-call(bf16[32,32,128]{2,1,0:T(8,128)(2,1)S(1)} %all-to-all-done.2.blocks_ref, bf16[3,4096,128]{2,1,0:T(8,128)(2,1)S(1)} %bitcast.17), custom_call_target="tpu_custom_call" | custom-call | tf_op jit(solution)/shard_map/merge/pallas_call | solution.py:181
  74.0 22.3 %all_gather.3.merged_ref = bf16[512,384]{1,0:T(8,128)(2,1)S(1)} all-gather(bf16[32,384]{1,0:T(8,128)(2,1)S(1)} %merge.1), channel_id=1, replica_groups=mesh['seq'=32,'rep'=16] {'rep'}, dimensions={0}, use_global_device_ids=true | all-gather | bytes 417792 | tf_op jit(solution)/shard_map/all_gather | solution.py:288
  96.4 0.0 all-to-all-done.1.square_ref
  96.4 1.8 %attend.1 = bf16[1024,128]{1,0:T(8,128)(2,1)S(1)} custom-call(f32[32,8,128]{2,1,0:T(8,128)S(1)} %all-to-all-done.1.square_ref, bf16[1024,512]{1,0:T(8,128)(2,1)S(1)} %bitcast.16, bf16[512,384]{1,0:T(8,128)(2,1)S(1)} %all_gather.3.merged_ref), custom_call_target="tpu_custom_call" | custom-call | tf_op jit(solution)/shard_map/attend/pallas_call | solution.py:260
  98.1 20.9 %all_to_all.35 = bf16[32,32,128]{2,1,0:T(8,128)(2,1)S(1)} all-to-all(bf16[32,32,128]{2,1,0:T(8,128)(2,1)S(1)} %bitcast.18), channel_id=1, replica_groups=mesh['seq'=32,'rep'=16] {'seq'}, dimensions={0} | all-to-all | bytes 524288 | tf_op jit(solution)/shard_map/all_to_all | solution.py:295
  119.1 0.7 copy_bitcast_fusion
Async XLA Ops:
  0.0 56.0 %copy-start.4 = (bf16[512,128]{1,0:T(8,128)(2,1)S(1)}, bf16[512,128]{1,0:T(8,128)(2,1)}, u32[]{:S(2)}) copy-start(bf16[512,128]{1,0:T(8,128)(2,1)} %weight_ref.3) | copy-start | bytes 393220
  1.6 5.8 %collective-permute-start = (bf16[64,512]{1,0:T(8,128)(2,1)}, bf16[64,512]{1,0:T(8,128)(2,1)S(1)}, u32[]{:S(2)}, u32[]{:S(2)}) collective-permute-start(bf16[64,512]{1,0:T(8,128)(2,1)} %get-tuple-element.15), channel_id=1, source_target_pairs={{16,0},{32,16},{48,32},{64,48},{80,64},{96,80},{112,96},{128,112},... | collective-permute-start | bytes 196616 | tf_op jit(solution)/shard_map/ppermute | solution.py:25
  3.6 0.9 copy-start.1
  4.5 1.0 copy-start.2
  5.6 0.7 copy-start.3
  49.1 17.2 %all-to-all-start.2 = ((bf16[32,32,128]{2,1,0:T(8,128)(2,1)}), bf16[32,32,128]{2,1,0:T(8,128)(2,1)S(1)}, u32[]{:S(2)}, u32[]{:S(2)}) async-start(bf16[32,32,128]{2,1,0:T(8,128)(2,1)} %get-tuple-element.18), calls=%async_computation.2 | async-start | bytes 524288 | tf_op jit(solution)/shard_map/all_to_all | solution.py:272
  67.0 29.3 %all-to-all-start.1 = ((f32[32,8,128]{2,1,0:T(8,128)}), f32[32,8,128]{2,1,0:T(8,128)S(1)}, u32[]{:S(2)}, u32[]{:S(2)}) async-start(f32[32,8,128]{2,1,0:T(8,128)} %broadcast_in_dim.8), calls=%async_computation.1 | async-start | bytes 262144 | tf_op jit(solution)/shard_map/all_to_all | solution.py:272
  70.9 1.9 %copy-start = (bf16[4096,3,128]{2,0,1:T(8,128)(2,1)S(1)}, bf16[4096,3,128]{2,0,1:T(8,128)(2,1)}, u32[]{:S(2)}) copy-start(bf16[4096,3,128]{2,0,1:T(8,128)(2,1)} %param.13) | copy-start | bytes 9437188

commit v8 on v7

--- a/solution.py
+++ b/solution.py
@@ -34,20 +34,18 @@
 
 
 def rows_kernel(index_ref, weight_ref, gain_ref, states_ref, out_ref, edge_ref):
-    block = (weight_ref[...].astype(jnp.float32) * gain_ref[...].astype(jnp.float32)).astype(
+    out_ref[...] = (weight_ref[...].astype(jnp.float32) * gain_ref[...].astype(jnp.float32)).astype(
         jnp.bfloat16
     )
-    for target in range(out_ref.shape[0]):
-        out_ref[target] = block
     edge_ref[...] = states_ref[...]
 
 
-def weight_rows(out_weight, norm_gain, states, index, copies):
+def weight_rows(out_weight, norm_gain, states, index):
     columns, width = out_weight.shape[1], states.shape[1]
     return pl.pallas_call(
         rows_kernel,
         out_shape=(
-            jax.ShapeDtypeStruct((copies, ROWS, columns), jnp.bfloat16),
+            jax.ShapeDtypeStruct((ROWS, columns), jnp.bfloat16),
             jax.ShapeDtypeStruct((HALO, width), jnp.bfloat16),
         ),
         grid_spec=pltpu.PrefetchScalarGridSpec(
@@ -59,7 +57,7 @@
                 pl.BlockSpec((HALO, width), lambda step, index: (0, 0)),
             ],
             out_specs=[
-                pl.BlockSpec((copies, ROWS, columns), lambda step, index: (0, 0, 0)),
+                pl.BlockSpec((ROWS, columns), lambda step, index: (0, 0)),
                 pl.BlockSpec((HALO, width), lambda step, index: (0, 0)),
             ],
         ),
@@ -107,7 +105,7 @@
     )(base.reshape(1), starts, straddle, states, key_weight)
 
 
-def pool_kernel(first_ref, end_ref, states_ref, halo_ref, keys_ref, weight_ref, out_ref):
+def pool_kernel(first_ref, end_ref, states_ref, halo_ref, keys_ref, weight_ref, rows_ref, out_ref):
     window = jnp.concatenate([states_ref[...], halo_ref[...]], axis=0)
     halo_keys = jnp.dot(
         halo_ref[...], weight_ref[...], preferred_element_type=jnp.float32
@@ -137,21 +135,21 @@
         pooled.append(
             jnp.dot(cross, window[:, part], preferred_element_type=jnp.float32).astype(jnp.bfloat16)
         )
-    block = jnp.concatenate(pooled, axis=1)
+    block = jnp.concatenate(pooled + [rows_ref[...]], axis=1)
     for target in range(out_ref.shape[0]):
         out_ref[target] = block
 
 
-def pool(first, end, states, halo, keys, key_weight, copies):
-    patches, width = first.shape[0], states.shape[1]
+def pool(first, end, states, halo, keys, key_weight, rows, copies):
+    patches, width = first.shape[0], states.shape[1] + rows.shape[1]
     return pl.pallas_call(
         pool_kernel,
         out_shape=jax.ShapeDtypeStruct((copies, patches, width), jnp.bfloat16),
-        in_specs=whole(6),
+        in_specs=whole(7),
         out_specs=pl.BlockSpec(memory_space=pltpu.VMEM),
         compiler_params=pltpu.CompilerParams(vmem_limit_bytes=16 << 20),
         name="pool",
-    )(first, end, states, halo, keys, key_weight)
+    )(first, end, states, halo, keys, key_weight, rows)
 
 
 def merge_kernel(blocks_ref, weight_ref, out_ref, total_ref):
@@ -173,17 +171,19 @@
 
 
 def merge_weights(blocks, attn_weight):
-    shards_total, block_rows, columns = blocks.shape
+    shards_total, _, carried = blocks.shape
     steps = 4
     group = shards_total // steps
     planes = jnp.swapaxes(attn_weight, 0, 1)
-    parts, _, width = planes.shape
+    parts, model_width, width = planes.shape
+    columns = model_width // shards_total
+    last = carried // columns - 1
     return pl.pallas_call(
         merge_kernel,
         out_shape=jax.ShapeDtypeStruct((ROWS, parts * width), jnp.bfloat16),
         grid=(steps,),
         in_specs=[
-            pl.BlockSpec((group, block_rows, columns), lambda s: (s, 0, 0)),
+            pl.BlockSpec((group, ROWS, columns), lambda s: (s, 0, last)),
             pl.BlockSpec((parts, group * columns, width), lambda s: (0, s, 0)),
         ],
         out_specs=pl.BlockSpec((ROWS, parts * width), lambda s: (0, 0)),
@@ -210,7 +210,8 @@
         rows = slice(tile * WIDE, (tile + 1) * WIDE)
         column = jnp.concatenate(columns[tile * WIDE // 128 : (tile + 1) * WIDE // 128], axis=0)
         view_ref[rows, :] = (
-            jnp.dot(pooled_ref[rows, :], merged_ref[...], preferred_element_type=jnp.float32)
+            jnp.dot(
+                pooled_ref[rows, : merged_ref.shape[0]], merged_ref[...], preferred_element_type=jnp.float32)
             * column
         ).astype(jnp.bfloat16)
     causal = lax.broadcasted_iota(jnp.int32, (TILE, TILE), 0) >= lax.broadcasted_iota(
@@ -278,20 +279,21 @@
     model_width = attn_weight.shape[0]
     pooled_width = out_weight.shape[0]
 
-    row_blocks, edge = weight_rows(out_weight, norm_gain, states, lax.axis_index("rep"), seq)
-    weight_blocks = exchange(row_blocks, "seq")
+    rows, edge = weight_rows(out_weight, norm_gain, states, lax.axis_index("rep"))
     halo_rows = shifted(edge, "seq", -1)
     keys, first, end, own, weight = own_keys(base, starts, straddle, states, key_weight)
-    pooled_blocks = pool(first, end, own, halo_rows, keys, weight, seq)
-    pooled_all = exchange(pooled_blocks, "seq").reshape(-1, pooled_width)
-    merged = merge_weights(weight_blocks, attn_weight)
-    merged_all = lax.all_gather(merged, "rep", axis=0, tiled=True)
+    blocks = pool(first, end, own, halo_rows, keys, weight, rows, seq)
+    blocks = exchange(blocks, "seq")
+    carried = blocks.reshape(-1, blocks.shape[2])
+    padded = jnp.pad(out_weight, ((0, carried.shape[1] - pooled_width), (0, 0)))
     part = lax.dot_general(
-        out_weight, pooled_all, (((0,), (1,)), ((), ())), preferred_element_type=jnp.float32
+        padded, carried, (((0,), (1,)), ((), ())), preferred_element_type=jnp.float32
     )
     part_square = jnp.sum(part * part, axis=0).reshape(-1, 128)
     square_all = exchange(jnp.broadcast_to(part_square[None], (seq,) + part_square.shape), "seq")
-    attended = attend(model_width, square_all, pooled_all, merged_all)
+    merged = merge_weights(blocks, attn_weight)
+    merged_all = lax.all_gather(merged, "rep", axis=0, tiled=True)
+    attended = attend(model_width, square_all, carried, merged_all)
     return lax.all_to_all(attended, "seq", split_axis=0, concat_axis=1, tiled=True)
 
 

time: 120 us -> 112 us (0.933)
  waiting for transfers between devices: 10.3 us -> 0.41 us
  blocking collectives: 83.3 us -> 89.7 us
  starting transfers between devices: 12 us -> 6.12 us
    all_to_all x2 -> x1, waiting for transfers between devices: 9.9 us -> 0.01 us  [exchange(): return lax.all_to_all(blocks, axis, split_axis=0, concat_axis=0, tiled=True)]
    all_to_all x1, blocking collectives: 40 us -> 48.1 us  [exchange(): return lax.all_to_all(blocks, axis, split_axis=0, concat_axis=0, tiled=True)]
    all_to_all x2 -> x1, starting transfers between devices: 10.7 us -> 4.84 us  [exchange(): return lax.all_to_all(blocks, axis, split_axis=0, concat_axis=0, tiled=True)]
    all_gather x1, blocking collectives: 22.3 us -> 20.7 us  [layer(): merged_all = lax.all_gather(merged, 'rep', axis=0, tiled=True)]
    unnamed x10 -> x12, local copies, waits for them, and re-layouts: 4.51 us -> 5.21 us
  transfers between devices with their start and end apart: 3 -> 2, of which waited for: 2 -> 1; matrix products, arithmetic and copies ran while one was open for 0% -> 0% of each run, Pallas kernels for 2% -> 2%
where the time goes in v8:
time: 112 us; the launch traced here: 111 us
  blocking collectives  89.7 us (80%)
  Pallas kernels  6.98 us (6%)
  local copies, waits for them, and re-layouts  6.59 us (6%)
  starting transfers between devices  6.12 us (5%)
    all_to_all x1, blocking collectives, exchange(): return lax.all_to_all(blocks, axis, split_axis=0, concat_axis=0, tiled=True)  48.1 us
    all_to_all x1, blocking collectives, layer(): lax.all_to_all(attended, 'seq', split_axis=0, concat_axis=1, tiled=True)  20.9 us
    all_gather x1, blocking collectives, layer(): merged_all = lax.all_gather(merged, 'rep', axis=0, tiled=True)  20.7 us
    unnamed x12, local copies, waits for them, and re-layouts  5.21 us
    all_to_all x1, starting transfers between devices, exchange(): return lax.all_to_all(blocks, axis, split_axis=0, concat_axis=0, tiled=True)  4.84 us
  transfers between devices with their start and end apart: 2, of which 1 were waited for; matrix products, arithmetic and copies ran while one was open for 0% of the time, Pallas kernels for 2%

profile of v8, /device:TPU:1, one launch (start us, length us, event | category | flops | bytes accessed | tf_op | source)
XLA Modules:
  0.0 111.1 jit_solution(15560971067289623150)
XLA Ops:
  0.0 1.5 %rows.1 = (bf16[32,128]{1,0:T(8,128)(2,1)}, bf16[64,512]{1,0:T(8,128)(2,1)}) custom-call(s32[1]{0:T(128)} %bitcast.1.index_ref, bf16[512,128]{1,0:T(8,128)(2,1)} %weight_ref.3, bf16[1,128]{1,0:T(2,128)(2,1)} %bitcast.19, bf16[192,512]{1,0:T(8,128)(2,1)} %states_ref.3), custom_call_target="tpu_custom_call" | custom-call | tf_op jit(solution)/shard_map/rows/pallas_call | solution.py:45
  1.5 1.3 %collective-permute-start = (bf16[64,512]{1,0:T(8,128)(2,1)}, bf16[64,512]{1,0:T(8,128)(2,1)S(1)}, u32[]{:S(2)}, u32[]{:S(2)}) collective-permute-start(bf16[64,512]{1,0:T(8,128)(2,1)} %get-tuple-element.15), channel_id=1, source_target_pairs={{16,0},{32,16},{48,32},{64,48},{80,64},{96,80},{112,96},{128,112},... | collective-permute-start | bytes 196616 | tf_op jit(solution)/shard_map/ppermute | solution.py:25
  3.4 0.0 copy-start.1
  3.5 0.9 copy-done.1
  4.4 0.0 copy-start.2
  4.4 1.0 copy-done.2
  5.4 0.0 copy-start.4
  5.4 0.7 copy-done.4
  6.1 0.8 own_keys.1
  6.9 0.4 collective-permute-done.halo_ref
  7.3 0.0 copy-start.3
  7.3 0.7 copy-done.3
  8.0 1.6 %pool.1 = bf16[32,32,640]{2,1,0:T(8,128)(2,1)S(1)} custom-call(s32[32,128]{1,0:T(8,128)S(1)} %get-tuple-element.12.first_ref, s32[32,128]{1,0:T(8,128)S(1)} %get-tuple-element.13.end_ref, bf16[192,512]{1,0:T(8,128)(2,1)S(1)} %get-tuple-element.14.states_ref, bf16[64,512]{1,0:T(8,128)(2,1)S(1)} %collective-permute-done.halo_ref, ...), custom_call_target="tpu_custom_call" | custom-call | tf_op jit(solution)/shard_map/pool/pallas_call | solution.py:145
  9.6 0.0 copy-start.5
  9.6 48.1 %all_to_all.29.blocks_ref = bf16[32,32,640]{2,1,0:T(8,128)(2,1)S(1)} all-to-all(bf16[32,32,640]{2,1,0:T(8,128)(2,1)S(1)} %pool.1), channel_id=1, replica_groups=mesh['seq'=32,'rep'=16] {'seq'}, dimensions={0} | all-to-all | bytes 2621440 | tf_op jit(solution)/shard_map/all_to_all | solution.py:273
  57.7 0.0 copy-done.5
  57.7 0.6 fusion
  58.3 0.7 broadcast_in_dim.8
  58.9 4.8 %all-to-all-start.1 = ((f32[32,8,128]{2,1,0:T(8,128)}), f32[32,8,128]{2,1,0:T(8,128)S(1)}, u32[]{:S(2)}, u32[]{:S(2)}) async-start(f32[32,8,128]{2,1,0:T(8,128)} %broadcast_in_dim.8), calls=%async_computation.1 | async-start | bytes 262144 | tf_op jit(solution)/shard_map/all_to_all | solution.py:273
  63.8 0.0 copy-start
  63.8 1.9 %copy-done = bf16[4096,3,128]{2,0,1:T(8,128)(2,1)S(1)} copy-done((bf16[4096,3,128]{2,0,1:T(8,128)(2,1)S(1)}, bf16[4096,3,128]{2,0,1:T(8,128)(2,1)}, u32[]{:S(2)}) %copy-start) | copy-done | bytes 3145752
  65.7 1.3 %merge.1 = bf16[32,384]{1,0:T(8,128)(2,1)S(1)} custom-call(bf16[32,32,640]{2,1,0:T(8,128)(2,1)S(1)} %all_to_all.29.blocks_ref, bf16[3,4096,128]{2,1,0:T(8,128)(2,1)S(1)} %bitcast.16), custom_call_target="tpu_custom_call" | custom-call | tf_op jit(solution)/shard_map/merge/pallas_call | solution.py:181
  67.0 20.7 %all_gather.3.merged_ref = bf16[512,384]{1,0:T(8,128)(2,1)S(1)} all-gather(bf16[32,384]{1,0:T(8,128)(2,1)S(1)} %merge.1), channel_id=1, replica_groups=mesh['seq'=32,'rep'=16] {'rep'}, dimensions={0}, use_global_device_ids=true | all-gather | bytes 417792 | tf_op jit(solution)/shard_map/all_gather | solution.py:295
  87.7 0.0 all-to-all-done.1.square_ref
  87.7 1.8 %attend.1 = bf16[1024,128]{1,0:T(8,128)(2,1)S(1)} custom-call(f32[32,8,128]{2,1,0:T(8,128)S(1)} %all-to-all-done.1.square_ref, bf16[1024,640]{1,0:T(8,128)(2,1)S(1)} %bitcast.15, bf16[512,384]{1,0:T(8,128)(2,1)S(1)} %all_gather.3.merged_ref), custom_call_target="tpu_custom_call" | custom-call | tf_op jit(solution)/shard_map/attend/pallas_call | solution.py:261
  89.4 20.9 %all_to_all.30 = bf16[32,32,128]{2,1,0:T(8,128)(2,1)S(1)} all-to-all(bf16[32,32,128]{2,1,0:T(8,128)(2,1)S(1)} %bitcast.17), channel_id=1, replica_groups=mesh['seq'=32,'rep'=16] {'seq'}, dimensions={0} | all-to-all | bytes 524288 | tf_op jit(solution)/shard_map/all_to_all | solution.py:297
  110.4 0.7 copy_bitcast_fusion
Async XLA Ops:
  1.5 5.8 %collective-permute-start = (bf16[64,512]{1,0:T(8,128)(2,1)}, bf16[64,512]{1,0:T(8,128)(2,1)S(1)}, u32[]{:S(2)}, u32[]{:S(2)}) collective-permute-start(bf16[64,512]{1,0:T(8,128)(2,1)} %get-tuple-element.15), channel_id=1, source_target_pairs={{16,0},{32,16},{48,32},{64,48},{80,64},{96,80},{112,96},{128,112},... | collective-permute-start | bytes 196616 | tf_op jit(solution)/shard_map/ppermute | solution.py:25
  3.4 0.9 copy-start.1
  4.4 1.0 copy-start.2
  5.4 0.7 copy-start.4
  7.3 0.7 copy-start.3
  9.6 48.1 %copy-start.5 = (bf16[512,128]{1,0:T(8,128)(2,1)S(1)}, bf16[512,128]{1,0:T(8,128)(2,1)}, u32[]{:S(2)}) copy-start(bf16[512,128]{1,0:T(8,128)(2,1)} %weight_ref.3) | copy-start | bytes 393220
  58.9 28.7 %all-to-all-start.1 = ((f32[32,8,128]{2,1,0:T(8,128)}), f32[32,8,128]{2,1,0:T(8,128)S(1)}, u32[]{:S(2)}, u32[]{:S(2)}) async-start(f32[32,8,128]{2,1,0:T(8,128)} %broadcast_in_dim.8), calls=%async_computation.1 | async-start | bytes 262144 | tf_op jit(solution)/shard_map/all_to_all | solution.py:273
  63.8 1.9 %copy-start = (bf16[4096,3,128]{2,0,1:T(8,128)(2,1)S(1)}, bf16[4096,3,128]{2,0,1:T(8,128)(2,1)}, u32[]{:S(2)}) copy-start(bf16[4096,3,128]{2,0,1:T(8,128)(2,1)} %param.13) | copy-start | bytes 9437188

commit v9 on v7

--- a/solution.py
+++ b/solution.py
@@ -268,8 +268,17 @@
     )(square_all, pooled_all, merged_all)
 
 
-def exchange(blocks, axis):
-    return lax.all_to_all(blocks, axis, split_axis=0, concat_axis=0, tiled=True)
+def exchange(blocks, axis, groups=None):
+    return lax.all_to_all(
+        blocks, axis, split_axis=0, concat_axis=0, tiled=True, axis_index_groups=groups
+    )
+
+
+def scattered(size):
+    order = [0]
+    while len(order) < size:
+        order = [2 * i for i in order] + [2 * i + 1 for i in order]
+    return order
 
 
 def layer(states, starts, straddle, key_weight, out_weight, norm_gain, attn_weight):
@@ -290,7 +299,8 @@
         out_weight, pooled_all, (((0,), (1,)), ((), ())), preferred_element_type=jnp.float32
     )
     part_square = jnp.sum(part * part, axis=0).reshape(-1, 128)
-    square_all = exchange(jnp.broadcast_to(part_square[None], (seq,) + part_square.shape), "seq")
+    copies = jnp.broadcast_to(part_square[None], (seq,) + part_square.shape)
+    square_all = exchange(copies, "seq", [scattered(seq)])
     attended = attend(model_width, square_all, pooled_all, merged_all)
     return lax.all_to_all(attended, "seq", split_axis=0, concat_axis=1, tiled=True)
 

time: 120 us -> 120 us (level)
  no operation moved by 1% of the time
where the time goes in v9:
time: 120 us
  blocking collectives  83.2 us (69%)
  starting transfers between devices  12 us (10%)
  waiting for transfers between devices  10.3 us (9%)
  Pallas kernels  7.11 us (6%)
  local copies, waits for them, and re-layouts  5.89 us (5%)
    all_to_all x1, blocking collectives, exchange(): lax.all_to_all(blocks, axis, split_axis=0, concat_axis=0, tiled=True, axi...  40 us
    all_gather x1, blocking collectives, layer(): merged_all = lax.all_gather(merged, 'rep', axis=0, tiled=True)  22.3 us
    all_to_all x1, blocking collectives, layer(): lax.all_to_all(attended, 'seq', split_axis=0, concat_axis=1, tiled=True)  20.9 us
    all_to_all x2, starting transfers between devices, exchange(): lax.all_to_all(blocks, axis, split_axis=0, concat_axis=0, tiled=True, axi...  10.7 us
    all_to_all x2, waiting for transfers between devices, exchange(): lax.all_to_all(blocks, axis, split_axis=0, concat_axis=0, tiled=True, axi...  9.9 us
    unnamed x10, local copies, waits for them, and re-layouts  4.51 us
  transfers between devices with their start and end apart: 3, of which 2 were waited for; matrix products, arithmetic and copies ran while one was open for 0% of the time, Pallas kernels for 2%

profile of v9, /device:TPU:1, one launch (start us, length us, event | category | flops | bytes accessed | tf_op | source)
XLA Modules:
  0.0 119.7 jit_solution(4600945214819766128)
XLA Ops:
  0.0 0.0 copy-start.4
  0.0 1.6 %rows.1 = (bf16[32,32,128]{2,1,0:T(8,128)(2,1)}, bf16[64,512]{1,0:T(8,128)(2,1)}) custom-call(s32[1]{0:T(128)} %bitcast.1.index_ref, bf16[512,128]{1,0:T(8,128)(2,1)} %weight_ref.3, bf16[1,128]{1,0:T(2,128)(2,1)} %bitcast.20, bf16[192,512]{1,0:T(8,128)(2,1)} %states_ref.3), custom_call_target="tpu_custom_call" | custom-call | tf_op jit(solution)/shard_map/rows/pallas_call | solution.py:47
  1.6 1.3 %collective-permute-start = (bf16[64,512]{1,0:T(8,128)(2,1)}, bf16[64,512]{1,0:T(8,128)(2,1)S(1)}, u32[]{:S(2)}, u32[]{:S(2)}) collective-permute-start(bf16[64,512]{1,0:T(8,128)(2,1)} %get-tuple-element.15), channel_id=1, source_target_pairs={{16,0},{32,16},{48,32},{64,48},{80,64},{96,80},{112,96},{128,112},... | collective-permute-start | bytes 196616 | tf_op jit(solution)/shard_map/ppermute | solution.py:25
  3.6 0.0 copy-start.1
  3.6 0.9 copy-done.1
  4.5 0.0 copy-start.2
  4.5 1.0 copy-done.2
  5.6 0.0 copy-start.3
  5.6 0.7 copy-done.3
  6.2 0.8 own_keys.1
  7.0 0.4 collective-permute-done.halo_ref
  7.4 1.7 %pool.1 = bf16[32,32,512]{2,1,0:T(8,128)(2,1)S(1)} custom-call(s32[32,128]{1,0:T(8,128)S(1)} %get-tuple-element.12.first_ref, s32[32,128]{1,0:T(8,128)S(1)} %get-tuple-element.13.end_ref, bf16[192,512]{1,0:T(8,128)(2,1)S(1)} %get-tuple-element.14.states_ref, bf16[64,512]{1,0:T(8,128)(2,1)S(1)} %collective-permute-done.halo_ref, ...), custom_call_target="tpu_custom_call" | custom-call | tf_op jit(solution)/shard_map/pool/pallas_call | solution.py:147
  9.1 40.0 %all_to_all.34 = bf16[32,32,512]{2,1,0:T(8,128)(2,1)S(1)} all-to-all(bf16[32,32,512]{2,1,0:T(8,128)(2,1)S(1)} %pool.1), channel_id=1, replica_groups=mesh['seq'=32,'rep'=16] {'seq'}, dimensions={0} | all-to-all | bytes 2097152 | tf_op jit(solution)/shard_map/all_to_all | solution.py:272
  49.1 6.8 %all-to-all-start.2 = ((bf16[32,32,128]{2,1,0:T(8,128)(2,1)}), bf16[32,32,128]{2,1,0:T(8,128)(2,1)S(1)}, u32[]{:S(2)}, u32[]{:S(2)}) async-start(bf16[32,32,128]{2,1,0:T(8,128)(2,1)} %get-tuple-element.18), calls=%async_computation.2 | async-start | bytes 524288 | tf_op jit(solution)/shard_map/all_to_all | solution.py:272
  56.0 0.0 copy-done.4
  56.0 0.5 fusion
  56.5 9.9 %all-to-all-done.2.blocks_ref = bf16[32,32,128]{2,1,0:T(8,128)(2,1)S(1)} async-done(((bf16[32,32,128]{2,1,0:T(8,128)(2,1)}), bf16[32,32,128]{2,1,0:T(8,128)(2,1)S(1)}, u32[]{:S(2)}, u32[]{:S(2)}) %all-to-all-start.2) | async-done | bytes 262176 | tf_op jit(solution)/shard_map/all_to_all | solution.py:272
  66.4 0.7 broadcast_in_dim.8
  67.0 3.9 %all-to-all-start.1 = ((f32[32,8,128]{2,1,0:T(8,128)}), f32[32,8,128]{2,1,0:T(8,128)S(1)}, u32[]{:S(2)}, u32[]{:S(2)}) async-start(f32[32,8,128]{2,1,0:T(8,128)} %broadcast_in_dim.8), calls=%async_computation.1 | async-start | bytes 262144 | tf_op jit(solution)/shard_map/all_to_all | solution.py:272
  70.9 0.0 copy-start
  70.9 1.9 %copy-done = bf16[4096,3,128]{2,0,1:T(8,128)(2,1)S(1)} copy-done((bf16[4096,3,128]{2,0,1:T(8,128)(2,1)S(1)}, bf16[4096,3,128]{2,0,1:T(8,128)(2,1)}, u32[]{:S(2)}) %copy-start) | copy-done | bytes 3145752
  72.8 1.2 %merge.1 = bf16[32,384]{1,0:T(8,128)(2,1)S(1)} custom-call(bf16[32,32,128]{2,1,0:T(8,128)(2,1)S(1)} %all-to-all-done.2.blocks_ref, bf16[3,4096,128]{2,1,0:T(8,128)(2,1)S(1)} %bitcast.17), custom_call_target="tpu_custom_call" | custom-call | tf_op jit(solution)/shard_map/merge/pallas_call | solution.py:181
  74.0 22.3 %all_gather.3.merged_ref = bf16[512,384]{1,0:T(8,128)(2,1)S(1)} all-gather(bf16[32,384]{1,0:T(8,128)(2,1)S(1)} %merge.1), channel_id=1, replica_groups=mesh['seq'=32,'rep'=16] {'rep'}, dimensions={0}, use_global_device_ids=true | all-gather | bytes 417792 | tf_op jit(solution)/shard_map/all_gather | solution.py:297
  96.4 0.0 all-to-all-done.1.square_ref
  96.4 1.8 %attend.1 = bf16[1024,128]{1,0:T(8,128)(2,1)S(1)} custom-call(f32[32,8,128]{2,1,0:T(8,128)S(1)} %all-to-all-done.1.square_ref, bf16[1024,512]{1,0:T(8,128)(2,1)S(1)} %bitcast.16, bf16[512,384]{1,0:T(8,128)(2,1)S(1)} %all_gather.3.merged_ref), custom_call_target="tpu_custom_call" | custom-call | tf_op jit(solution)/shard_map/attend/pallas_call | solution.py:260
  98.1 20.9 %all_to_all.35 = bf16[32,32,128]{2,1,0:T(8,128)(2,1)S(1)} all-to-all(bf16[32,32,128]{2,1,0:T(8,128)(2,1)S(1)} %bitcast.18), channel_id=1, replica_groups=mesh['seq'=32,'rep'=16] {'seq'}, dimensions={0} | all-to-all | bytes 524288 | tf_op jit(solution)/shard_map/all_to_all | solution.py:305
  119.0 0.7 copy_bitcast_fusion
Async XLA Ops:
  0.0 56.0 %copy-start.4 = (bf16[512,128]{1,0:T(8,128)(2,1)S(1)}, bf16[512,128]{1,0:T(8,128)(2,1)}, u32[]{:S(2)}) copy-start(bf16[512,128]{1,0:T(8,128)(2,1)} %weight_ref.3) | copy-start | bytes 393220
  1.6 5.8 %collective-permute-start = (bf16[64,512]{1,0:T(8,128)(2,1)}, bf16[64,512]{1,0:T(8,128)(2,1)S(1)}, u32[]{:S(2)}, u32[]{:S(2)}) collective-permute-start(bf16[64,512]{1,0:T(8,128)(2,1)} %get-tuple-element.15), channel_id=1, source_target_pairs={{16,0},{32,16},{48,32},{64,48},{80,64},{96,80},{112,96},{128,112},... | collective-permute-start | bytes 196616 | tf_op jit(solution)/shard_map/ppermute | solution.py:25
  3.6 0.9 copy-start.1
  4.5 1.0 copy-start.2
  5.6 0.7 copy-start.3
  49.1 17.2 %all-to-all-start.2 = ((bf16[32,32,128]{2,1,0:T(8,128)(2,1)}), bf16[32,32,128]{2,1,0:T(8,128)(2,1)S(1)}, u32[]{:S(2)}, u32[]{:S(2)}) async-start(bf16[32,32,128]{2,1,0:T(8,128)(2,1)} %get-tuple-element.18), calls=%async_computation.2 | async-start | bytes 524288 | tf_op jit(solution)/shard_map/all_to_all | solution.py:272
  67.0 29.3 %all-to-all-start.1 = ((f32[32,8,128]{2,1,0:T(8,128)}), f32[32,8,128]{2,1,0:T(8,128)S(1)}, u32[]{:S(2)}, u32[]{:S(2)}) async-start(f32[32,8,128]{2,1,0:T(8,128)} %broadcast_in_dim.8), calls=%async_computation.1 | async-start | bytes 262144 | tf_op jit(solution)/shard_map/all_to_all | solution.py:272
  70.9 1.9 %copy-start = (bf16[4096,3,128]{2,0,1:T(8,128)(2,1)S(1)}, bf16[4096,3,128]{2,0,1:T(8,128)(2,1)}, u32[]{:S(2)}) copy-start(bf16[4096,3,128]{2,0,1:T(8,128)(2,1)} %param.13) | copy-start | bytes 9437188

commit v10 on v9

--- a/solution.py
+++ b/solution.py
@@ -154,40 +154,22 @@
     )(first, end, states, halo, keys, key_weight)
 
 
-def merge_kernel(blocks_ref, weight_ref, out_ref, total_ref):
-    step = pl.program_id(0)
-
-    @pl.when(step == 0)
-    def _():
-        total_ref[...] = jnp.zeros_like(total_ref)
-
-    rows = jnp.concatenate([blocks_ref[shard] for shard in range(blocks_ref.shape[0])], axis=1)
+def merge_kernel(order, blocks_ref, weight_ref, out_ref):
+    rows = jnp.concatenate([blocks_ref[order.index(shard)] for shard in range(len(order))], axis=1)
     for part in range(weight_ref.shape[0]):
-        total_ref[:, part * HD : (part + 1) * HD] += jnp.dot(
+        out_ref[:, part * HD : (part + 1) * HD] = jnp.dot(
             rows, weight_ref[part], preferred_element_type=jnp.float32
-        )
-
-    @pl.when(step == pl.num_programs(0) - 1)
-    def _():
-        out_ref[...] = total_ref[...].astype(jnp.bfloat16)
+        ).astype(jnp.bfloat16)
 
 
 def merge_weights(blocks, attn_weight):
-    shards_total, block_rows, columns = blocks.shape
-    steps = 4
-    group = shards_total // steps
     planes = jnp.swapaxes(attn_weight, 0, 1)
     parts, _, width = planes.shape
     return pl.pallas_call(
-        merge_kernel,
+        functools.partial(merge_kernel, scattered(blocks.shape[0])),
         out_shape=jax.ShapeDtypeStruct((ROWS, parts * width), jnp.bfloat16),
-        grid=(steps,),
-        in_specs=[
-            pl.BlockSpec((group, block_rows, columns), lambda s: (s, 0, 0)),
-            pl.BlockSpec((parts, group * columns, width), lambda s: (0, s, 0)),
-        ],
-        out_specs=pl.BlockSpec((ROWS, parts * width), lambda s: (0, 0)),
-        scratch_shapes=[pltpu.VMEM((ROWS, parts * width), jnp.float32)],
+        in_specs=whole(2),
+        out_specs=pl.BlockSpec(memory_space=pltpu.VMEM),
         compiler_params=pltpu.CompilerParams(vmem_limit_bytes=16 << 20),
         name="merge",
     )(blocks, planes)
@@ -217,7 +199,6 @@
         jnp.int32, (TILE, TILE), 1
     )
     scale = jnp.float32(HD**-0.5)
-
     def against(tile, first, last):
         return lax.dot_general(
             view_ref[tile * TILE : (tile + 1) * TILE, :HD],
@@ -288,7 +269,7 @@
     pooled_width = out_weight.shape[0]
 
     row_blocks, edge = weight_rows(out_weight, norm_gain, states, lax.axis_index("rep"), seq)
-    weight_blocks = exchange(row_blocks, "seq")
+    weight_blocks = exchange(row_blocks, "seq", [scattered(seq)])
     halo_rows = shifted(edge, "seq", -1)
     keys, first, end, own, weight = own_keys(base, starts, straddle, states, key_weight)
     pooled_blocks = pool(first, end, own, halo_rows, keys, weight, seq)
@@ -300,7 +281,7 @@
     )
     part_square = jnp.sum(part * part, axis=0).reshape(-1, 128)
     copies = jnp.broadcast_to(part_square[None], (seq,) + part_square.shape)
-    square_all = exchange(copies, "seq", [scattered(seq)])
+    square_all = exchange(copies, "seq")
     attended = attend(model_width, square_all, pooled_all, merged_all)
     return lax.all_to_all(attended, "seq", split_axis=0, concat_axis=1, tiled=True)
 

time: 120 us -> 120 us (level)
  transfers between devices with their start and end apart: 3 -> 3, of which waited for: 2 -> 2; matrix products, arithmetic and copies ran while one was open for 0% -> 0% of each run, Pallas kernels for 2% -> 1%
where the time goes in v10:
time: 120 us
  blocking collectives  83.1 us (69%)
  starting transfers between devices  12 us (10%)
  waiting for transfers between devices  11 us (9%)
  Pallas kernels  6.45 us (5%)
  local copies, waits for them, and re-layouts  5.89 us (5%)
    all_to_all x1, blocking collectives, exchange(): lax.all_to_all(blocks, axis, split_axis=0, concat_axis=0, tiled=True, axi...  40 us
    all_gather x1, blocking collectives, layer(): merged_all = lax.all_gather(merged, 'rep', axis=0, tiled=True)  22.1 us
    all_to_all x1, blocking collectives, layer(): lax.all_to_all(attended, 'seq', split_axis=0, concat_axis=1, tiled=True)  20.9 us
    all_to_all x2, starting transfers between devices, exchange(): lax.all_to_all(blocks, axis, split_axis=0, concat_axis=0, tiled=True, axi...  10.7 us
    all_to_all x2, waiting for transfers between devices, exchange(): lax.all_to_all(blocks, axis, split_axis=0, concat_axis=0, tiled=True, axi...  10.5 us
    unnamed x10, local copies, waits for them, and re-layouts  4.51 us
  transfers between devices with their start and end apart: 3, of which 2 were waited for; matrix products, arithmetic and copies ran while one was open for 0% of the time, Pallas kernels for 1%

profile of v10, /device:TPU:1, one launch (start us, length us, event | category | flops | bytes accessed | tf_op | source)
XLA Modules:
  0.0 119.6 jit_solution(13007337064309699592)
XLA Ops:
  0.0 0.0 copy-start.4
  0.0 1.6 %rows.1 = (bf16[32,32,128]{2,1,0:T(8,128)(2,1)}, bf16[64,512]{1,0:T(8,128)(2,1)}) custom-call(s32[1]{0:T(128)} %bitcast.1.index_ref, bf16[512,128]{1,0:T(8,128)(2,1)} %weight_ref.3, bf16[1,128]{1,0:T(2,128)(2,1)} %bitcast.20, bf16[192,512]{1,0:T(8,128)(2,1)} %states_ref.3), custom_call_target="tpu_custom_call" | custom-call | tf_op jit(solution)/shard_map/rows/pallas_call | solution.py:47
  1.6 1.3 %collective-permute-start = (bf16[64,512]{1,0:T(8,128)(2,1)}, bf16[64,512]{1,0:T(8,128)(2,1)S(1)}, u32[]{:S(2)}, u32[]{:S(2)}) collective-permute-start(bf16[64,512]{1,0:T(8,128)(2,1)} %get-tuple-element.15), channel_id=1, source_target_pairs={{16,0},{32,16},{48,32},{64,48},{80,64},{96,80},{112,96},{128,112},... | collective-permute-start | bytes 196616 | tf_op jit(solution)/shard_map/ppermute | solution.py:25
  3.6 0.0 copy-start.1
  3.6 0.9 copy-done.1
  4.5 0.0 copy-start.2
  4.5 1.0 copy-done.2
  5.6 0.0 copy-start.3
  5.6 0.7 copy-done.3
  6.2 0.8 own_keys.1
  7.0 0.4 collective-permute-done.halo_ref
  7.4 1.7 %pool.1 = bf16[32,32,512]{2,1,0:T(8,128)(2,1)S(1)} custom-call(s32[32,128]{1,0:T(8,128)S(1)} %get-tuple-element.12.first_ref, s32[32,128]{1,0:T(8,128)S(1)} %get-tuple-element.13.end_ref, bf16[192,512]{1,0:T(8,128)(2,1)S(1)} %get-tuple-element.14.states_ref, bf16[64,512]{1,0:T(8,128)(2,1)S(1)} %collective-permute-done.halo_ref, ...), custom_call_target="tpu_custom_call" | custom-call | tf_op jit(solution)/shard_map/pool/pallas_call | solution.py:147
  9.1 40.0 %all_to_all.34 = bf16[32,32,512]{2,1,0:T(8,128)(2,1)S(1)} all-to-all(bf16[32,32,512]{2,1,0:T(8,128)(2,1)S(1)} %pool.1), channel_id=1, replica_groups=mesh['seq'=32,'rep'=16] {'seq'}, dimensions={0} | all-to-all | bytes 2097152 | tf_op jit(solution)/shard_map/all_to_all | solution.py:253
  49.1 6.8 %all-to-all-start.2 = ((bf16[32,32,128]{2,1,0:T(8,128)(2,1)}), bf16[32,32,128]{2,1,0:T(8,128)(2,1)S(1)}, u32[]{:S(2)}, u32[]{:S(2)}) async-start(bf16[32,32,128]{2,1,0:T(8,128)(2,1)} %get-tuple-element.18), calls=%async_computation.2 | async-start | bytes 524288 | tf_op jit(solution)/shard_map/all_to_all | solution.py:253
  56.0 0.0 copy-done.4
  56.0 0.5 fusion
  56.5 10.5 %all-to-all-done.2.blocks_ref = bf16[32,32,128]{2,1,0:T(8,128)(2,1)S(1)} async-done(((bf16[32,32,128]{2,1,0:T(8,128)(2,1)}), bf16[32,32,128]{2,1,0:T(8,128)(2,1)S(1)}, u32[]{:S(2)}, u32[]{:S(2)}) %all-to-all-start.2) | async-done | bytes 262176 | tf_op jit(solution)/shard_map/all_to_all | solution.py:253
  67.0 0.7 broadcast_in_dim.8
  67.7 3.9 %all-to-all-start.1 = ((f32[32,8,128]{2,1,0:T(8,128)}), f32[32,8,128]{2,1,0:T(8,128)S(1)}, u32[]{:S(2)}, u32[]{:S(2)}) async-start(f32[32,8,128]{2,1,0:T(8,128)} %broadcast_in_dim.8), calls=%async_computation.1 | async-start | bytes 262144 | tf_op jit(solution)/shard_map/all_to_all | solution.py:253
  71.6 0.0 copy-start
  71.6 1.9 %copy-done = bf16[4096,3,128]{2,0,1:T(8,128)(2,1)S(1)} copy-done((bf16[4096,3,128]{2,0,1:T(8,128)(2,1)S(1)}, bf16[4096,3,128]{2,0,1:T(8,128)(2,1)}, u32[]{:S(2)}) %copy-start) | copy-done | bytes 3145752
  73.4 0.6 merge.1
  74.0 22.1 %all_gather.3.merged_ref = bf16[512,384]{1,0:T(8,128)(2,1)S(1)} all-gather(bf16[32,384]{1,0:T(8,128)(2,1)S(1)} %merge.1), channel_id=1, replica_groups=mesh['seq'=32,'rep'=16] {'rep'}, dimensions={0}, use_global_device_ids=true | all-gather | bytes 417792 | tf_op jit(solution)/shard_map/all_gather | solution.py:278
  96.2 0.0 all-to-all-done.1.square_ref
  96.2 1.8 %attend.1 = bf16[1024,128]{1,0:T(8,128)(2,1)S(1)} custom-call(f32[32,8,128]{2,1,0:T(8,128)S(1)} %all-to-all-done.1.square_ref, bf16[1024,512]{1,0:T(8,128)(2,1)S(1)} %bitcast.16, bf16[512,384]{1,0:T(8,128)(2,1)S(1)} %all_gather.3.merged_ref), custom_call_target="tpu_custom_call" | custom-call | tf_op jit(solution)/shard_map/attend/pallas_call | solution.py:241
  97.9 20.9 %all_to_all.35 = bf16[32,32,128]{2,1,0:T(8,128)(2,1)S(1)} all-to-all(bf16[32,32,128]{2,1,0:T(8,128)(2,1)S(1)} %bitcast.18), channel_id=1, replica_groups=mesh['seq'=32,'rep'=16] {'seq'}, dimensions={0} | all-to-all | bytes 524288 | tf_op jit(solution)/shard_map/all_to_all | solution.py:286
  118.9 0.7 copy_bitcast_fusion
Async XLA Ops:
  0.0 56.0 %copy-start.4 = (bf16[512,128]{1,0:T(8,128)(2,1)S(1)}, bf16[512,128]{1,0:T(8,128)(2,1)}, u32[]{:S(2)}) copy-start(bf16[512,128]{1,0:T(8,128)(2,1)} %weight_ref.3) | copy-start | bytes 393220
  1.6 5.8 %collective-permute-start = (bf16[64,512]{1,0:T(8,128)(2,1)}, bf16[64,512]{1,0:T(8,128)(2,1)S(1)}, u32[]{:S(2)}, u32[]{:S(2)}) collective-permute-start(bf16[64,512]{1,0:T(8,128)(2,1)} %get-tuple-element.15), channel_id=1, source_target_pairs={{16,0},{32,16},{48,32},{64,48},{80,64},{96,80},{112,96},{128,112},... | collective-permute-start | bytes 196616 | tf_op jit(solution)/shard_map/ppermute | solution.py:25
  3.6 0.9 copy-start.1
  4.5 1.0 copy-start.2
  5.6 0.7 copy-start.3
  49.1 17.9 %all-to-all-start.2 = ((bf16[32,32,128]{2,1,0:T(8,128)(2,1)}), bf16[32,32,128]{2,1,0:T(8,128)(2,1)S(1)}, u32[]{:S(2)}, u32[]{:S(2)}) async-start(bf16[32,32,128]{2,1,0:T(8,128)(2,1)} %get-tuple-element.18), calls=%async_computation.2 | async-start | bytes 524288 | tf_op jit(solution)/shard_map/all_to_all | solution.py:253
  67.7 28.5 %all-to-all-start.1 = ((f32[32,8,128]{2,1,0:T(8,128)}), f32[32,8,128]{2,1,0:T(8,128)S(1)}, u32[]{:S(2)}, u32[]{:S(2)}) async-start(f32[32,8,128]{2,1,0:T(8,128)} %broadcast_in_dim.8), calls=%async_computation.1 | async-start | bytes 262144 | tf_op jit(solution)/shard_map/all_to_all | solution.py:253
  71.6 1.9 %copy-start = (bf16[4096,3,128]{2,0,1:T(8,128)(2,1)S(1)}, bf16[4096,3,128]{2,0,1:T(8,128)(2,1)}, u32[]{:S(2)}) copy-start(bf16[4096,3,128]{2,0,1:T(8,128)(2,1)} %param.13) | copy-start | bytes 9437188
